TPU v7x, 256 devices: a whole 4x4x8 slice. The times are simulated.
256 devices in a mesh: lon: 32 (over y, z), lat: 8 (over x, core).
Axes of the slice: x: 4, y: 4, z: 8, core: 2. Of those that a mesh axis runs over, the one named last changes fastest.
Arguments:
- forcing: float32 [512, 8192], P('lat', 'lon'), may hold values from -27 to 27
- surface_term: float32 [512, 8192], P('lat', 'lon'), may hold values from 0.001 to 0.025
- sea_cells: int32 [512, 8192], P('lat', 'lon'), may hold values from 0 to 1, as said below
- levels: int32 [512, 8192], P('lat', 'lon'), may hold values from 4 to 60
Outputs:
- solution: float32 [512, 8192], P('lat', 'lon')
- residual: float32 [512, 8192], P('lat', 'lon')
Inputs may be any that keep to these rules, and one draw needn't show every extreme that they name: `sea_cells`: land (0) lies only at cells whose row and longitude index, counted from 0, are both even.
All inputs are finite; a program needn't handle non-finite values.
Results may differ from a plain program's by a relative error of at most 0.0003.
Values sent between devices are 32-bit elements; how exact they have to be, the bound alone decides.
A program may use at most 64 MiB of HBM per device.

v0:
```python
import jax
import jax.numpy as jnp
from jax import lax
from jax.sharding import PartitionSpec as P

LEVELS = 3
SWEEPS = 2
BOTTOM_ITERS = 6


DAMPING = 0.8
ROW_STEP = 150.0 / 8640.0
BAND_SOUTH = -50.0


def with_halo(block, sides, width, periodic):
    for axis, dim in sides:
        count = lax.axis_size(axis)
        forward = [(i, i + 1) for i in range(count - 1)]
        if periodic:
            forward.append((count - 1, 0))
        backward = [(target, source) for source, target in forward]
        low = lax.ppermute(
            lax.slice_in_dim(block, block.shape[dim] - width, None, axis=dim), axis, forward
        )
        high = lax.ppermute(lax.slice_in_dim(block, 0, width, axis=dim), axis, backward)
        block = jnp.concatenate([low, block, high], axis=dim)
    return block


def depth_of(levels, sea_mask):
    layers = levels.astype(jnp.float32)
    return sea_mask * ((layers + layers * (layers - 1.0) / 20.0) / 200.0)


def metric(first_row, row_count):
    row_index = first_row + jnp.arange(row_count, dtype=jnp.float32)[:, None]
    center = jnp.cos(jnp.deg2rad(BAND_SOUTH + ROW_STEP * (row_index + 0.5)))
    northern = jnp.cos(jnp.deg2rad(BAND_SOUTH + ROW_STEP * (row_index + 1.0)))
    return (center, northern)


def stencil(field, east_val, west_val, north_val, south_val, coeffs):
    return coeffs[4] * field - (
        coeffs[0] * east_val + coeffs[1] * west_val + coeffs[2] * north_val + coeffs[3] * south_val
    )


def coarsen(east_face, north_face, source_term, sea_mask):
    east_next = east_face[0::2, 1::2] + east_face[1::2, 1::2]
    north_next = north_face[1::2, 0::2] + north_face[1::2, 1::2]
    source_next = (
        source_term[0::2, 0::2]
        + source_term[1::2, 0::2]
        + source_term[0::2, 1::2]
        + source_term[1::2, 1::2]
    )
    mask_next = jnp.maximum(
        jnp.maximum(sea_mask[0::2, 0::2], sea_mask[1::2, 0::2]),
        jnp.maximum(sea_mask[0::2, 1::2], sea_mask[1::2, 1::2]),
    )
    return (east_next, north_next, source_next, mask_next)


def restrict(field):
    return field[0::2, 0::2] + field[1::2, 0::2] + field[0::2, 1::2] + field[1::2, 1::2]


def prolong(field, sea_mask):
    return jnp.repeat(jnp.repeat(field, 2, axis=0), 2, axis=1) * sea_mask


def with_diagonal(east_face, west_face, north_face, south_face, source_term, sea_mask):
    diagonal = sea_mask * (source_term + east_face + west_face + north_face + south_face) + (
        1.0 - sea_mask
    )
    return (east_face, west_face, north_face, south_face, diagonal, 1.0 / diagonal)


def with_rims(stacked):
    widened = with_halo(stacked, (("lon", 2),), 1, True)
    return with_halo(widened, (("lat", 1),), 1, False)


def apply_grid(field, coeffs):
    padded = with_rims(field[None])[0]
    return stencil(
        field, padded[1:-1, 2:], padded[1:-1, :-2], padded[2:, 1:-1], padded[:-2, 1:-1], coeffs
    )


def finish(east_face, north_face, source_term, sea_mask):
    padded = with_rims(jnp.stack([east_face, north_face]))
    west_face = padded[0, 1:-1, :-2]
    south_face = padded[1, :-2, 1:-1]
    return with_diagonal(east_face, west_face, north_face, south_face, source_term, sea_mask)


def smooth(field, source, coeffs):
    return field + DAMPING * coeffs[5] * (source - apply_grid(field, coeffs))


def conjugate(source, coeffs, apply_fn, total_fn):
    iterate = jnp.zeros_like(source)
    remain = source
    direction = source
    norm_now = total_fn(jnp.sum(remain * remain))
    for sweep_index in range(BOTTOM_ITERS):
        image = apply_fn(direction, coeffs)
        step_size = norm_now / total_fn(jnp.sum(direction * image))
        iterate = iterate + step_size * direction
        remain = remain - step_size * image
        norm_next = total_fn(jnp.sum(remain * remain))
        direction = remain + norm_next / norm_now * direction
        norm_now = norm_next
    return iterate


def grid_total(value):
    return lax.psum(value, ("lon", "lat"))


def on_device(forcing, surface_term, sea_cells, levels):
    row_count = forcing.shape[0]
    first_row = (lax.axis_index("lat") * row_count).astype(jnp.float32)
    sea_mask = sea_cells.astype(jnp.float32)
    depth = depth_of(levels, sea_mask)
    center, northern = metric(first_row, row_count)
    padded = with_rims(depth[None])[0]
    east_face = jnp.minimum(depth, padded[1:-1, 2:]) / center
    north_face = jnp.minimum(depth, padded[2:, 1:-1]) * northern
    source_term = surface_term * center * sea_mask
    coeff_list = []
    mask_list = []
    for level_index in range(LEVELS + 1):
        coeff_list.append(finish(east_face, north_face, source_term, sea_mask))
        mask_list.append(sea_mask)
        if level_index < LEVELS:
            east_face, north_face, source_term, sea_mask = coarsen(
                east_face, north_face, source_term, sea_mask
            )
    source = forcing * mask_list[0]
    first_source = source
    sources = []
    iterates = []
    for level_index in range(LEVELS):
        coeffs = coeff_list[level_index]
        field = DAMPING * coeffs[5] * source
        field = smooth(field, source, coeffs)
        image = apply_grid(field, coeffs)
        sources.append(source)
        iterates.append(field)
        source = restrict(source - image)
    coeffs = coeff_list[LEVELS]
    correction = conjugate(source, coeffs, apply_grid, grid_total)
    for level_index in range(LEVELS - 1, -1, -1):
        coeffs = coeff_list[level_index]
        field = iterates[level_index] + prolong(correction, mask_list[level_index])
        for sweep_index in range(SWEEPS):
            field = smooth(field, sources[level_index], coeffs)
        correction = field
    residual = first_source - apply_grid(correction, coeff_list[0])
    return (correction, residual)


def solution(mesh):
    return jax.shard_map(
        on_device,
        mesh=mesh,
        in_specs=(P("lat", "lon"), P("lat", "lon"), P("lat", "lon"), P("lat", "lon")),
        out_specs=(P("lat", "lon"), P("lat", "lon")),
        check_vma=False,
    )
```

profile of v0, /device:TPU:1, one launch (start us, length us, event | category | flops | bytes accessed | tf_op | source)
XLA Modules:
  0.0 1187.8 jit_solution(16993836291310737523)
XLA Ops:
  1.8 8.9 collective-permute-start.1
  11.4 5.0 collective-permute-done
  49.1 5.3 collective-permute-start.38
  63.2 6.4 collective-permute-start.9
  78.8 5.0 collective-permute-done.14
  131.1 5.0 collective-permute-done.29
  138.3 5.1 collective-permute-start.31
  152.7 5.4 collective-permute-start.35
  167.7 5.4 collective-permute-start.42
  174.8 74.3 %all-reduce = (f32[]{:T(128)}, f32[]{:T(128)}) all-reduce(f32[]{:T(128)} %get-tuple-element.11, f32[]{:T(128)} %get-tuple-element.10), channel_id=1, replica_groups=mesh['lon'=32,'lat'=8] {'lon','lat'}, use_global_device_ids=true, to_apply=%region_1.0 | all-reduce | flops 2 | bytes 16 | tf_op jit(solution)/shard_map/psum | solution.py:120
  251.0 73.5 %psum.86 = f32[]{:T(128)} all-reduce(f32[]{:T(128)} %multiply_reduce_fusion.8), channel_id=1, replica_groups=mesh['lon'=32,'lat'=8] {'lon','lat'}, use_global_device_ids=true, to_apply=%region_5.0 | all-reduce | flops 1 | bytes 8 | tf_op jit(solution)/shard_map/psum | solution.py:120
  328.7 5.2 collective-permute-done.44
  341.9 72.9 %psum.87 = f32[]{:T(128)} all-reduce(f32[]{:T(128)} %get-tuple-element.26), channel_id=1, replica_groups=mesh['lon'=32,'lat'=8] {'lon','lat'}, use_global_device_ids=true, to_apply=%region_7.0 | all-reduce | flops 1 | bytes 8 | tf_op jit(solution)/shard_map/psum | solution.py:120
  416.7 73.5 %psum.88 = f32[]{:T(128)} all-reduce(f32[]{:T(128)} %get-tuple-element.24), channel_id=1, replica_groups=mesh['lon'=32,'lat'=8] {'lon','lat'}, use_global_device_ids=true, to_apply=%region_9.0 | all-reduce | flops 1 | bytes 8 | tf_op jit(solution)/shard_map/psum | solution.py:120
  494.2 5.0 collective-permute-done.48
  507.2 72.9 %psum.89 = f32[]{:T(128)} all-reduce(f32[]{:T(128)} %get-tuple-element.22), channel_id=1, replica_groups=mesh['lon'=32,'lat'=8] {'lon','lat'}, use_global_device_ids=true, to_apply=%region_11.0 | all-reduce | flops 1 | bytes 8 | tf_op jit(solution)/shard_map/psum | solution.py:120
  582.0 73.5 %psum.90 = f32[]{:T(128)} all-reduce(f32[]{:T(128)} %get-tuple-element.20), channel_id=1, replica_groups=mesh['lon'=32,'lat'=8] {'lon','lat'}, use_global_device_ids=true, to_apply=%region_13.0 | all-reduce | flops 1 | bytes 8 | tf_op jit(solution)/shard_map/psum | solution.py:120
  659.6 5.0 collective-permute-done.52
  672.5 72.9 %psum.91 = f32[]{:T(128)} all-reduce(f32[]{:T(128)} %get-tuple-element.18), channel_id=1, replica_groups=mesh['lon'=32,'lat'=8] {'lon','lat'}, use_global_device_ids=true, to_apply=%region_15.0 | all-reduce | flops 1 | bytes 8 | tf_op jit(solution)/shard_map/psum | solution.py:120
  747.4 73.5 %psum.92 = f32[]{:T(128)} all-reduce(f32[]{:T(128)} %get-tuple-element.16), channel_id=1, replica_groups=mesh['lon'=32,'lat'=8] {'lon','lat'}, use_global_device_ids=true, to_apply=%region_17.0 | all-reduce | flops 1 | bytes 8 | tf_op jit(solution)/shard_map/psum | solution.py:120
  824.9 5.0 collective-permute-done.56
  837.9 72.9 %psum.93 = f32[]{:T(128)} all-reduce(f32[]{:T(128)} %get-tuple-element.14), channel_id=1, replica_groups=mesh['lon'=32,'lat'=8] {'lon','lat'}, use_global_device_ids=true, to_apply=%region_19.0 | all-reduce | flops 1 | bytes 8 | tf_op jit(solution)/shard_map/psum | solution.py:120
  912.7 73.5 %psum.94 = f32[]{:T(128)} all-reduce(f32[]{:T(128)} %multiply_reduce_fusion), channel_id=1, replica_groups=mesh['lon'=32,'lat'=8] {'lon','lat'}, use_global_device_ids=true, to_apply=%region_21.0 | all-reduce | flops 1 | bytes 8 | tf_op jit(solution)/shard_map/psum | solution.py:120
  990.5 5.0 collective-permute-done.60
  1003.5 72.9 %psum.95 = f32[]{:T(128)} all-reduce(f32[]{:T(128)} %fusion.113), channel_id=1, replica_groups=mesh['lon'=32,'lat'=8] {'lon','lat'}, use_global_device_ids=true, to_apply=%region_23.0 | all-reduce | flops 1 | bytes 8 | tf_op jit(solution)/shard_map/psum | solution.py:120
  1080.7 5.0 collective-permute-done.64
  1102.4 5.0 collective-permute-start.70
  1116.9 5.4 collective-permute-start.74
  1131.8 5.4 collective-permute-start.78
  1147.1 5.4 collective-permute-start.82
  1163.0 5.5 collective-permute-start.86
  1178.8 5.5 collective-permute-start.90
  (391 shorter events, 250.2 us)
Async XLA Ops:
  1.8 9.6 collective-permute-start.1
  16.6 10.7 collective-permute-start.3
  31.5 10.3 collective-permute-start.4
  31.6 10.2 collective-permute-start.5
  36.6 39.7 %collective-permute-start.11 = (f32[2,32,1]{2,1,0:T(8,128)S(1)}, f32[2,32,1]{2,1,0:T(8,128)S(1)}, u32[]{:S(2)}, u32[]{:S(2)}) collective-permute-start(f32[2,32,1]{2,1,0:T(8,128)S(1)} %get-tuple-element.110), channel_id=1, source_target_pairs={{0,8},{8,16},{16,24},{24,32},{32,40},{40,48},{48,56},{56,64},{64,7... | collective-permute-start | bytes 776 | tf_op jit(solution)/shard_map/ppermute | solution.py:23
  36.6 41.5 %collective-permute-start.12 = (f32[2,32,1]{2,1,0:T(8,128)S(1)}, f32[2,32,1]{2,1,0:T(8,128)S(1)}, u32[]{:S(2)}, u32[]{:S(2)}) collective-permute-start(f32[2,32,1]{2,1,0:T(8,128)S(1)} %get-tuple-element.109), channel_id=1, source_target_pairs={{8,0},{16,8},{24,16},{32,24},{40,32},{48,40},{56,48},{64,56},{72,6... | collective-permute-start | bytes 776 | tf_op jit(solution)/shard_map/ppermute | solution.py:26
  41.6 57.5 %collective-permute-start.22 = (f32[2,16,1]{2,1,0:T(8,128)S(1)}, f32[2,16,1]{2,1,0:T(8,128)S(1)}, u32[]{:S(2)}, u32[]{:S(2)}) collective-permute-start(f32[2,16,1]{2,1,0:T(8,128)S(1)} %get-tuple-element.136), channel_id=1, source_target_pairs={{0,8},{8,16},{16,24},{24,32},{32,40},{40,48},{48,56},{56,64},{64,7... | collective-permute-start | bytes 392 | tf_op jit(solution)/shard_map/ppermute | solution.py:23
  41.9 7.1 collective-permute-start.6
  45.8 8.7 collective-permute-start.37
  61.2 9.1 collective-permute-start.10
  63.2 8.9 collective-permute-start.9
  70.3 28.8 %collective-permute-start.23 = (f32[2,16,1]{2,1,0:T(8,128)S(1)}, f32[2,16,1]{2,1,0:T(8,128)S(1)}, u32[]{:S(2)}, u32[]{:S(2)}) collective-permute-start(f32[2,16,1]{2,1,0:T(8,128)S(1)} %get-tuple-element.135), channel_id=1, source_target_pairs={{8,0},{16,8},{24,16},{32,24},{40,32},{48,40},{56,48},{64,56},{72,6... | collective-permute-start | bytes 392 | tf_op jit(solution)/shard_map/ppermute | solution.py:26
  72.1 102.0 %collective-permute-start.39 = (f32[2,1,34]{1,2,0:T(8,128)S(1)}, f32[2,1,34]{1,2,0:T(8,128)S(1)}, u32[]{:S(2)}, u32[]{:S(2)}) collective-permute-start(f32[2,1,34]{1,2,0:T(8,128)S(1)} %slice.974), channel_id=1, source_target_pairs={{0,1},{1,2},{2,3},{3,4},{4,5},{5,6},{6,7},{8,9},{9,10},{10,11},{11... | collective-permute-start | bytes 824 | tf_op jit(solution)/shard_map/ppermute | solution.py:23
  83.9 8.5 collective-permute-start.17
  85.9 8.7 collective-permute-start.16
  103.6 7.0 collective-permute-start.21
  111.8 6.8 collective-permute-start.26
  113.7 14.6 %collective-permute-start.24 = (f32[2,1,66]{1,2,0:T(8,128)S(1)}, f32[2,1,66]{1,2,0:T(8,128)S(1)}, u32[]{:S(2)}, u32[]{:S(2)}) collective-permute-start(f32[2,1,66]{1,2,0:T(8,128)S(1)} %copy.160), channel_id=1, source_target_pairs={{0,1},{1,2},{2,3},{3,4},{4,5},{5,6},{6,7},{8,9},{9,10},{10,11},{11... | collective-permute-start | bytes 1592 | tf_op jit(solution)/shard_map/ppermute | solution.py:23
  118.7 8.6 collective-permute-start.28
  136.2 7.7 collective-permute-start.32
  150.7 7.6 collective-permute-start.36
  165.8 7.4 collective-permute-start.43
  1085.9 7.0 collective-permute-start.67
  1100.1 7.3 collective-permute-start.71
  1114.9 7.4 collective-permute-start.75
  1129.9 7.4 collective-permute-start.79
  1145.1 8.1 collective-permute-start.83
  1147.1 7.4 collective-permute-start.82
  1161.1 8.2 collective-permute-start.87
  1163.0 7.5 collective-permute-start.86
  1176.9 8.2 collective-permute-start.91
  1178.8 7.5 collective-permute-start.90
  (63 other events, 282.9 us)
where the time goes:
time: 1200 us; the launch traced here: 1190 us
  blocking collectives  806 us (67%)
  starting transfers between devices  211 us (18%)
  waiting for transfers between devices  119 us (10%)
  local copies, waits for them, and re-layouts  22.1 us (2%)
  between operations  17.5 us (1%)
  other arithmetic  13.1 us (1%)
    psum x11, blocking collectives, grid_total(): return lax.psum(value, ('lon', 'lat'))  806 us
    ppermute x48, starting transfers between devices, with_halo(): lax.ppermute(lax.slice_in_dim(block, block.shape[dim] - width, None, axis...  112 us
    ppermute x48, waiting for transfers between devices, with_halo(): lax.ppermute(lax.slice_in_dim(block, block.shape[dim] - width, None, axis...  100 us
    ppermute x44, starting transfers between devices, with_halo(): lax.ppermute(lax.slice_in_dim(block, 0, width, axis=dim), axis, backward)  98.4 us
  transfers between devices with their start and end apart: 92, of which 59 were waited for; matrix products, arithmetic and copies ran while one was open for 1% of the time, Pallas kernels for 0%

commit v1 on v0

v1 whole, which is shorter than its diff:
```python
import functools
import math

import jax
import jax.numpy as jnp
from jax import lax
from jax.experimental import pallas as pl
from jax.experimental.pallas import tpu as pltpu
from jax.sharding import PartitionSpec as P

MESH = pl.DeviceIdType.MESH
DAMPING = 0.8
ROW_STEP = 150.0 / 8640.0
BAND_SOUTH = -50.0
BAND_ROWS = 512
BOTTOM_ITERS = 6
CORES = 2
RING = 8

ROWS, COLS = 64, 256
RIM = 32
PAD = 8
LANES = 128
CHUNK = 32


def lane_of(rows):
    return lax.broadcasted_iota(jnp.int32, (rows, LANES), 1)


def east_of(cols, shift, lane):
    count = len(cols)
    return [
        pltpu.roll(jnp.where(lane < shift, cols[(c + 1) % count], cols[c]), LANES - shift, 1)
        for c in range(count)
    ]


def west_of(cols, shift, lane):
    count = len(cols)
    return [
        pltpu.roll(jnp.where(lane >= LANES - shift, cols[(c - 1) % count], cols[c]), shift, 1)
        for c in range(count)
    ]


def pair_sum(value, shift, lane):
    upper = (lane & shift) != 0
    return value + jnp.where(upper, pltpu.roll(value, shift, 1), pltpu.roll(value, LANES - shift, 1))


def upper_of(value, shift, lane):
    return jnp.where((lane & shift) != 0, value, pltpu.roll(value, LANES - shift, 1))


def cosines(row):
    middle = math.radians(BAND_SOUTH + ROW_STEP * (BAND_ROWS / 2))
    off = (row - BAND_ROWS / 2) * math.radians(ROW_STEP)
    sq = off * off
    cos_off = 1.0 - sq * (1.0 / 2 - sq * (1.0 / 24 - sq * (1.0 / 720)))
    sin_off = off * (1.0 - sq * (1.0 / 6 - sq * (1.0 / 120 - sq * (1.0 / 5040))))
    return math.cos(middle) * cos_off - math.sin(middle) * sin_off


class Level:
    def __init__(self, index, refs):
        self.index = index
        self.shift = 1 << index
        self.rows = (ROWS + 2 * RIM) >> index
        self.rim = RIM >> index
        self.east, self.west, self.north, self.source, self.diag, self.scale, self.rhs, self.va, self.vb, self.tmp = refs
        self.chunk = min(CHUNK, self.rows)

    def chunks(self):
        return range(0, self.rows, self.chunk)

    def load(self, ref, col, row, count):
        return ref[col, pl.ds(PAD + row, count), :]

    def apply(self, ref, row, count, cols=3):
        lane = lane_of(count)
        value = [self.load(ref, c, row, count) for c in range(3)]
        east = east_of(value, self.shift, lane)
        west = west_of(value, self.shift, lane)
        out = []
        for c in range(cols):
            around = (
                self.load(self.east, c, row, count) * east[c]
                + self.load(self.west, c, row, count) * west[c]
                + self.load(self.north, c, row, count) * self.load(ref, c, row + 1, count)
                + self.load(self.north, c, row - 1, count) * self.load(ref, c, row - 1, count)
            )
            out.append(self.load(self.diag, c, row, count) * value[c] - around)
        return value, out

    def smooth(self, source_ref, target_ref):
        for row in self.chunks():
            value, image = self.apply(source_ref, row, self.chunk)
            for c in range(3):
                rest = self.load(self.rhs, c, row, self.chunk) - image[c]
                target_ref[c, pl.ds(PAD + row, self.chunk), :] = (
                    value[c] + self.load(self.scale, c, row, self.chunk) * rest
                )

    def finish(self):
        n = self.chunk
        lane = lane_of(n)
        for row in self.chunks():
            east = [self.load(self.east, c, row, n) for c in range(3)]
            west = west_of(east, self.shift, lane)
            for c in range(3):
                source = self.load(self.source, c, row, n)
                total = (
                    source + east[c] + west[c]
                    + self.load(self.north, c, row, n) + self.load(self.north, c, row - 1, n)
                )
                diag = jnp.where(source > 0.0, total, 1.0)
                self.west[c, pl.ds(PAD + row, n), :] = west[c]
                self.diag[c, pl.ds(PAD + row, n), :] = diag
                self.scale[c, pl.ds(PAD + row, n), :] = DAMPING / diag

    def pairs(self, ref, col, row, count):
        return (
            ref[col, pl.ds(PAD + 2 * row, count, stride=2), :],
            ref[col, pl.ds(PAD + 2 * row + 1, count, stride=2), :],
        )

    def coarse_faces(self, col, row, count):
        lane = lane_of(count)
        lower, upper = self.pairs(self.east, col, row, count)
        east = upper_of(lower + upper, self.shift, lane)
        _, upper = self.pairs(self.north, col, row, count)
        north = pair_sum(upper, self.shift, lane)
        lower, upper = self.pairs(self.source, col, row, count)
        return east, north, pair_sum(lower + upper, self.shift, lane)

    def coarse_rhs(self, col, row, count):
        lower, upper = self.pairs(self.tmp, col, row, count)
        return pair_sum(lower + upper, self.shift, lane_of(count))

    def descend(self):
        n = self.chunk
        for row in self.chunks():
            for c in range(3):
                self.vb[c, pl.ds(PAD + row, n), :] = self.load(self.scale, c, row, n) * self.load(self.rhs, c, row, n)
        self.smooth(self.vb, self.va)
        for row in self.chunks():
            _, image = self.apply(self.va, row, n)
            for c in range(3):
                self.tmp[c, pl.ds(PAD + row, n), :] = self.load(self.rhs, c, row, n) - image[c]

    def rise(self, coarse, offset, masked):
        half = self.rows // 2
        n = min(CHUNK, half)
        for row in range(0, half, n):
            for c in range(3):
                added = coarse[c, pl.ds(offset + row, n), :]
                for odd in range(2):
                    at = pl.ds(PAD + 2 * row + odd, n, stride=2)
                    own = jnp.where(self.source[c, at, :] > 0.0, added, 0.0) if masked else added
                    self.va[c, at, :] = self.va[c, at, :] + own
        self.smooth(self.va, self.vb)
        self.smooth(self.vb, self.va)


def body(
    shape, forcing, surface, sea, depth_levels, solution_out, residual_out,
    in_f, in_i, fields, *rest
):
    lat_count, lon_count, ring = shape
    level_refs = [rest[0:7], rest[7:17], rest[17:27]]
    (
        west_pack, east_pack, east_rim, west_rim, metric,
        face_slots, rhs_slots, faces, rhs, bottom, wide, piece,
        in_sem, out_sem, rim_send, rim_recv, slot_send, slot_recv,
        plane_send, plane_recv, pass_send, pass_recv,
    ) = rest[27:]
    planes_y = lon_count // ring
    planes_x = lat_count // CORES
    la, lo = lax.axis_index("lat"), lax.axis_index("lon")
    x, core = la // CORES, la % CORES
    y, z = lo // ring, lo % ring
    tiles = lon_count * (COLS >> 3) // LANES
    own_rows = ROWS >> 3
    group = LANES // (COLS >> 3)

    depth = fields.at[0]
    levels = [
        Level(0, (*level_refs[0][0:3], fields.at[2], *level_refs[0][3:5], fields.at[1], *level_refs[0][5:7], wide)),
        Level(1, level_refs[1]),
        Level(2, level_refs[2]),
    ]

    def device(lat, lon):
        return {"lat": lat, "lon": lon}

    loads = []
    for k, ref in enumerate((forcing, surface)):
        for c in range(2):
            loads.append(pltpu.make_async_copy(ref.at[:, pl.ds(c * LANES, LANES)], in_f.at[k, c], in_sem))
    for k, ref in enumerate((sea, depth_levels)):
        for c in range(2):
            loads.append(pltpu.make_async_copy(ref.at[:, pl.ds(c * LANES, LANES)], in_i.at[k, c], in_sem))
    for load in loads:
        load.start()

    rims = [(dy, dx) for dy in (-1, 0, 1) for dx in (-1, 0, 1) if (dy, dx) != (0, 0)]
    hops = sorted(
        ((dx, dy) for dx in range(planes_x) for dy in range(planes_y) if (dx, dy) != (0, 0)),
        key=lambda d: min(d[0], planes_x - d[0]) + min(d[1], planes_y - d[1]),
    )
    barrier = pltpu.get_barrier_semaphore()

    def greet(lat, lon):
        pl.semaphore_signal(barrier, inc=1, device_id=device(lat, lon), device_id_type=MESH)

    def beside(dy, dx):
        return la + dy, lax.rem(lo + dx + lon_count, lon_count)

    def ring_peer(step):
        return la, y * ring + lax.rem(z + step, ring)

    def plane_peer(dx, dy):
        return lax.rem(x + dx, planes_x) * CORES + core, lax.rem(y + dy, planes_y) * ring + z

    partner = (x * CORES + (1 - core), lo)
    inside = {-1: la > 0, 0: None, 1: la < lat_count - 1}

    def where_inside(dy, act):
        if dy == 0:
            act()
        else:
            pl.when(inside[dy])(act)

    for dy, dx in rims:
        where_inside(dy, lambda dy=dy, dx=dx: greet(*beside(dy, dx)))
    for step in range(1, ring):
        greet(*ring_peer(step))
    for dx, dy in hops:
        greet(*plane_peer(dx, dy))
    greet(*partner)

    def clear(ref, col, row, count):
        ref[col, pl.ds(row, count), :] = jnp.zeros((count, LANES), ref.dtype)

    for k in range(3):
        clear_to = fields.at[k]
        for c in range(3):
            clear(clear_to, c, 0, PAD)
            clear(clear_to, c, PAD + ROWS + 2 * RIM, PAD)
    for level in levels:
        for ref in (level.north, level.va, level.vb):
            for c in range(3):
                clear(ref, c, 0, PAD)
                clear(ref, c, PAD + level.rows, PAD)
    for ref in (faces.at[1], rhs, bottom.at[0]):
        for t in range(tiles):
            clear(ref, t, 0, PAD)
            clear(ref, t, PAD + lat_count * own_rows, PAD)
    for dy, row in ((-1, 0), (1, RIM + ROWS)):

        @pl.when(jnp.logical_not(inside[dy]))
        def _(row=row):
            for k in range(3):
                for c in range(2):
                    clear(fields.at[k], c, PAD + row, RIM)
            east_rim[pl.ds(row, RIM), :] = jnp.zeros((RIM, LANES), jnp.float32)
            west_rim[pl.ds(row, RIM), :] = jnp.zeros((RIM, LANES), jnp.float32)

    first = la * ROWS - RIM
    for row in range(0, ROWS + 2 * RIM, CHUNK):
        number = (first + row + lax.broadcasted_iota(jnp.int32, (CHUNK, LANES), 0)).astype(jnp.float32)
        metric[0, pl.ds(row, CHUNK), :] = cosines(number + 0.5)
        metric[1, pl.ds(row, CHUNK), :] = cosines(number + 1.0)

    for load in loads:
        load.wait()
    for row in range(0, ROWS, CHUNK):
        at = pl.ds(PAD + RIM + row, CHUNK)
        center = metric[0, pl.ds(RIM + row, CHUNK), :]
        own = pl.ds(row, CHUNK)
        lane = lane_of(CHUNK)
        values = []
        for c in range(2):
            sea_mask = in_i[0, c, own, :].astype(jnp.float32)
            layers = in_i[1, c, own, :].astype(jnp.float32)
            deep = sea_mask * ((layers + layers * (layers - 1.0) / 20.0) / 200.0)
            right = in_f[0, c, own, :] * sea_mask
            source = in_f[1, c, own, :] * center * sea_mask
            values.append((deep, right, source))
            for k in range(3):
                fields[k, c, at, :] = values[c][k]
        packed_west, packed_east = values[0][0], values[1][0]
        for k in range(1, 3):
            part = (lane >= RIM * k) & (lane < RIM * (k + 1))
            packed_west = jnp.where(part, pltpu.roll(values[0][k], RIM * k, 1), packed_west)
            part = (lane < LANES - RIM * k) & (lane >= LANES - RIM * (k + 1))
            packed_east = jnp.where(part, pltpu.roll(values[1][k], LANES - RIM * k, 1), packed_east)
        west_pack[own, :] = packed_west
        east_pack[own, :] = packed_east

    greeted = 2 + (ring - 1) + len(hops) + 1
    both = inside[-1].astype(jnp.int32) + inside[1].astype(jnp.int32)
    pl.semaphore_wait(barrier, greeted + 3 * both)

    def rim_copy(dy, dx):
        source_row, target_row = {1: (ROWS - RIM, 0), -1: (0, RIM + ROWS), 0: (0, RIM)}[dy]
        count = ROWS if dy == 0 else RIM
        if dx == 0:
            source = fields.at[:, pl.ds(0, 2), pl.ds(PAD + RIM + source_row, count), :]
            target = fields.at[:, pl.ds(0, 2), pl.ds(PAD + target_row, count), :]
        else:
            source = (east_pack if dx > 0 else west_pack).at[pl.ds(source_row, count), :]
            target = (west_rim if dx > 0 else east_rim).at[pl.ds(target_row, count), :]
        k = rims.index((dy, dx))
        return pltpu.make_async_remote_copy(
            source, target, rim_send.at[k], rim_recv.at[k],
            device_id=device(*beside(dy, dx)), device_id_type=MESH,
        )

    order = sorted(rims, key=lambda d: (d[1] == 0, d[0] == 0))
    for dy, dx in order:
        where_inside(dy, lambda dy=dy, dx=dx: rim_copy(dy, dx).start())
    for dy, dx in order:
        where_inside(-dy, lambda dy=dy, dx=dx: rim_copy(dy, dx).wait_recv())

    for row in range(0, ROWS + 2 * RIM, CHUNK):
        lane = lane_of(CHUNK)
        east, west = east_rim[pl.ds(row, CHUNK), :], west_rim[pl.ds(row, CHUNK), :]
        for k in range(3):
            moved_east = pltpu.roll(east, LANES - RIM * k, 1) if k else east
            moved_west = pltpu.roll(west, RIM * k, 1) if k else west
            fields[k, 2, pl.ds(PAD + row, CHUNK), :] = jnp.where(
                lane < RIM, moved_east, jnp.where(lane >= LANES - RIM, moved_west, 0.0)
            )

    top = levels[0]
    for row in top.chunks():
        n = top.chunk
        deep = [top.load(depth, c, row, n) for c in range(3)]
        east = east_of(deep, 1, lane_of(n))
        inverse = 1.0 / metric[0, pl.ds(row, n), :]
        northern = metric[1, pl.ds(row, n), :]
        for c in range(3):
            at = pl.ds(PAD + row, n)
            top.east[c, at, :] = jnp.minimum(deep[c], east[c]) * inverse
            top.north[c, at, :] = jnp.minimum(deep[c], top.load(depth, c, row + 1, n)) * northern
    for fine, coarse in zip(levels, levels[1:]):
        for row in coarse.chunks():
            for c in range(3):
                at = pl.ds(PAD + row, coarse.chunk)
                coarse.east[c, at, :], coarse.north[c, at, :], coarse.source[c, at, :] = fine.coarse_faces(c, row, coarse.chunk)

    lane = lane_of(own_rows)
    pick = (lane % 16) * 8
    low = (lane % 32) < 16

    def dense(west_tile, east_tile):
        return jnp.where(
            low, jnp.take_along_axis(west_tile, pick, axis=1), jnp.take_along_axis(east_tile, pick, axis=1)
        )

    own3 = RIM >> 3
    bottom_faces = [levels[2].coarse_faces(c, own3, own_rows) for c in range(2)]
    parts = [dense(bottom_faces[0][k], bottom_faces[1][k]) for k in range(3)]
    face_slots[z] = jnp.where(lane < 32, parts[0], jnp.where(lane < 64, parts[1], parts[2]))

    def slot_copy(slots, which, step):
        return pltpu.make_async_remote_copy(
            slots.at[z], slots.at[z], slot_send.at[which], slot_recv.at[which],
            device_id=device(*ring_peer(step)), device_id_type=MESH,
        )

    def all_slots(slots, which):
        return pltpu.make_async_remote_copy(
            slots.at[pl.ds(0, ring - 1)], slots.at[pl.ds(0, ring - 1)], slot_send.at[which], slot_recv.at[which],
            device_id=device(*ring_peer(1)), device_id_type=MESH,
        )

    def plane_block(which, lat, line):
        rows = pl.ds(pl.multiple_of(PAD + lat * own_rows, 8), own_rows)
        per_line = tiles // planes_y
        if which == 0:
            return faces.at[:, pl.ds(line * per_line, per_line), rows, :]
        return rhs.at[pl.ds(line * per_line, per_line), rows, :]

    def plane_copy(which, k, dx, dy):
        block = plane_block(which, la, y)
        return pltpu.make_async_remote_copy(
            block, block, plane_send.at[which, k], plane_recv.at[which, k],
            device_id=device(*plane_peer(dx, dy)), device_id_type=MESH,
        )

    def pass_copy(which, lat, line):
        block = plane_block(which, lat, line)
        return pltpu.make_async_remote_copy(
            block, block, pass_send.at[which], pass_recv.at[which],
            device_id=device(*partner), device_id_type=MESH,
        )

    def all_passed(which):
        half = pl.ds(PAD, lat_count * own_rows // CORES)
        block = faces.at[:, :, half, :] if which == 0 else rhs.at[:, half, :]
        return pltpu.make_async_remote_copy(
            block, block, pass_send.at[which], pass_recv.at[which],
            device_id=device(*partner), device_id_type=MESH,
        )

    def send_plane(which):
        for k, (dx, dy) in enumerate(hops):
            plane_copy(which, k, dx, dy).start()
        pass_copy(which, la, y).start()

    def take_plane(which):
        for k, (dx, dy) in enumerate(hops):
            plane_copy(which, k, dx, dy).wait_recv()
            pass_copy(which, *(lax.rem(x - dx + planes_x, planes_x) * CORES + core, lax.rem(y - dy + planes_y, planes_y))).start()

    for step in range(1, ring):
        slot_copy(face_slots, 0, step).start()

    levels[0].finish()
    levels[0].descend()

    all_slots(face_slots, 0).wait_recv()
    per_line = tiles // planes_y
    own_at = pl.ds(pl.multiple_of(PAD + la * own_rows, 8), own_rows)
    for h in range(per_line):
        for k in range(3):
            value = None
            for j in range(group):
                slot = face_slots[h * group + j]
                shift = (32 * (j - k)) % LANES
                moved = pltpu.roll(slot, shift, 1) if shift else slot
                value = moved if value is None else jnp.where(lane // 32 == j, moved, value)
            faces[k, y * per_line + h, own_at, :] = value
    send_plane(0)

    for fine, coarse in zip(levels, levels[1:]):
        for row in coarse.chunks():
            for c in range(3):
                coarse.rhs[c, pl.ds(PAD + row, coarse.chunk), :] = fine.coarse_rhs(c, row, coarse.chunk)
        coarse.finish()
        coarse.descend()

    bottom_rhs = [levels[2].coarse_rhs(c, own3, own_rows) for c in range(2)]
    rhs_slots[z] = dense(*bottom_rhs)
    for step in range(1, ring):
        slot_copy(rhs_slots, 1, step).start()
    all_slots(rhs_slots, 1).wait_recv()
    for h in range(per_line):
        value = None
        for j in range(group):
            slot = rhs_slots[h * group + j]
            value = slot if value is None else jnp.where(lane // 32 == j, slot, value)
        rhs[y * per_line + h, own_at, :] = value
    send_plane(1)
    take_plane(0)
    take_plane(1)

    height = lat_count * own_rows
    everything = pl.ds(PAD, height)
    lane3 = lane_of(height)
    west_face, diagonal = bottom.at[1], bottom.at[2]
    rest_ref, image_ref, along_ref = bottom.at[0], bottom.at[3], bottom.at[4]
    all_passed(0).wait_recv()
    for t in range(tiles):
        east = faces[0, t, everything, :]
        before = faces[0, (t - 1) % tiles, everything, :]
        west = pltpu.roll(jnp.where(lane3 >= LANES - 1, before, east), 1, 1)
        west_face[t, everything, :] = west
        diagonal[t, everything, :] = (
            faces[2, t, everything, :] + east + west
            + faces[1, t, everything, :] + faces[1, t, pl.ds(PAD - 1, height), :]
        )
    all_passed(1).wait_recv()

    def operate(ref):
        norm, product = None, None
        for t in range(tiles):
            value = ref[t, everything, :]
            east = pltpu.roll(jnp.where(lane3 < 1, ref[(t + 1) % tiles, everything, :], value), LANES - 1, 1)
            west = pltpu.roll(jnp.where(lane3 >= LANES - 1, ref[(t - 1) % tiles, everything, :], value), 1, 1)
            image = diagonal[t, everything, :] * value - (
                faces[0, t, everything, :] * east
                + west_face[t, everything, :] * west
                + faces[1, t, everything, :] * ref[t, pl.ds(PAD + 1, height), :]
                + faces[1, t, pl.ds(PAD - 1, height), :] * ref[t, pl.ds(PAD - 1, height), :]
            )
            image_ref[t, everything, :] = image
            square, mixed = value * value, value * image
            norm = square if norm is None else norm + square
            product = mixed if product is None else product + mixed
        return jnp.sum(norm, keepdims=True), jnp.sum(product, keepdims=True)

    own_tile = lo // group
    near_tiles = (lax.rem(own_tile - 1 + tiles, tiles), own_tile, lax.rem(own_tile + 1, tiles))
    near = pl.ds(pl.multiple_of(la * own_rows, 8), 2 * PAD + own_rows)
    solved = [None] * 3
    direction = [None] * 3
    norm, product = operate(rhs)
    alpha = norm / product
    beta = None
    for iteration in range(BOTTOM_ITERS):
        current = rhs if iteration == 0 else rest_ref
        for k in range(3):
            value = current[near_tiles[k], near, :]
            direction[k] = value if iteration == 0 else value + beta * direction[k]
            solved[k] = alpha * direction[k] if iteration == 0 else solved[k] + alpha * direction[k]
        if iteration == BOTTOM_ITERS - 1:
            break
        for t in range(tiles):
            along = image_ref[t, everything, :]
            if iteration:
                along = along + beta * along_ref[t, everything, :]
            along_ref[t, everything, :] = along
            rest_ref[t, everything, :] = current[t, everything, :] - alpha * along
        norm_next, product = operate(rest_ref)
        beta = norm_next / norm
        alpha = norm_next / (product - beta * norm_next / alpha)
        norm = norm_next

    quarter = (lo % group) * 32
    lane = lane_of(8)
    place = quarter + jnp.where(lane < LANES // 2, 32 + lane // 8, (lane - LANES) // 8)
    wrapped = place & (LANES - 1)
    for row in range(0, 2 * PAD + own_rows, 8):
        left, mine, right = (solved[k][row : row + 8] for k in range(3))
        piece[0, pl.ds(row, 8), :] = jnp.take_along_axis(mine, quarter + lane // 8, axis=1)
        piece[1, pl.ds(row, 8), :] = jnp.take_along_axis(mine, quarter + 16 + lane // 8, axis=1)
        piece[2, pl.ds(row, 8), :] = jnp.where(
            place < 0, jnp.take_along_axis(left, wrapped, axis=1),
            jnp.where(place >= LANES, jnp.take_along_axis(right, wrapped, axis=1), jnp.take_along_axis(mine, wrapped, axis=1)),
        )

    levels[2].rise(piece, PAD - own3, False)
    levels[1].rise(levels[2].va, PAD, False)
    levels[0].rise(levels[1].va, PAD, True)
    stores = []
    for c in range(2):
        stores.append(pltpu.make_async_copy(
            top.va.at[c, pl.ds(PAD + RIM, ROWS), :], solution_out.at[:, pl.ds(c * LANES, LANES)], out_sem))
        stores[-1].start()
    for row in range(RIM, RIM + ROWS, CHUNK):
        _, image = top.apply(top.va, row, CHUNK, cols=2)
        for c in range(2):
            top.tmp[c, pl.ds(PAD + row, CHUNK), :] = top.load(top.rhs, c, row, CHUNK) - image[c]
    for c in range(2):
        stores.append(pltpu.make_async_copy(
            top.tmp.at[c, pl.ds(PAD + RIM, ROWS), :], residual_out.at[:, pl.ds(c * LANES, LANES)], out_sem))
        stores[-1].start()

    for dy, dx in order:
        where_inside(dy, lambda dy=dy, dx=dx: rim_copy(dy, dx).wait_send())
    for which, slots in enumerate((face_slots, rhs_slots)):
        all_slots(slots, which).wait_send()
        for k, (dx, dy) in enumerate(hops):
            plane_copy(which, k, dx, dy).wait_send()
        all_passed(which).wait_send()
    for store in stores:
        store.wait()


def solution(mesh, ring=RING):
    lat_count, lon_count = mesh.shape["lat"], mesh.shape["lon"]
    planes = (lat_count // CORES) * (lon_count // ring)
    tiles = lon_count * (COLS >> 3) // LANES
    height = lat_count * (ROWS >> 3) + 2 * PAD
    f32 = jnp.float32

    def padded(level):
        return pltpu.VMEM((3, ((ROWS + 2 * RIM) >> level) + 2 * PAD, LANES), f32)

    rows = ROWS + 2 * RIM
    scratch = [
        pltpu.VMEM((2, 2, ROWS, LANES), f32),
        pltpu.VMEM((2, 2, ROWS, LANES), jnp.int32),
        pltpu.VMEM((3, 3, rows + 2 * PAD, LANES), f32),
        *[padded(0)] * 7,
        *[padded(1)] * 10,
        *[padded(2)] * 10,
        pltpu.VMEM((ROWS, LANES), f32),
        pltpu.VMEM((ROWS, LANES), f32),
        pltpu.VMEM((rows, LANES), f32),
        pltpu.VMEM((rows, LANES), f32),
        pltpu.VMEM((2, rows, LANES), f32),
        pltpu.VMEM((ring, 8, LANES), f32),
        pltpu.VMEM((ring, 8, LANES), f32),
        pltpu.VMEM((3, tiles, height, LANES), f32),
        pltpu.VMEM((tiles, height, LANES), f32),
        pltpu.VMEM((5, tiles, height, LANES), f32),
        padded(0),
        pltpu.VMEM((3, 2 * PAD + (ROWS >> 3), LANES), f32),
        pltpu.SemaphoreType.DMA,
        pltpu.SemaphoreType.DMA,
        pltpu.SemaphoreType.DMA((8,)),
        pltpu.SemaphoreType.DMA((8,)),
        pltpu.SemaphoreType.DMA((2,)),
        pltpu.SemaphoreType.DMA((2,)),
        pltpu.SemaphoreType.DMA((2, planes)),
        pltpu.SemaphoreType.DMA((2, planes)),
        pltpu.SemaphoreType.DMA((2,)),
        pltpu.SemaphoreType.DMA((2,)),
    ]

    def step(forcing, surface_term, sea_cells, levels):
        out = jax.ShapeDtypeStruct(forcing.shape, f32)
        return pl.pallas_call(
            functools.partial(body, (lat_count, lon_count, ring)),
            out_shape=(out, out),
            in_specs=[pl.BlockSpec(memory_space=pl.ANY)] * 4,
            out_specs=[pl.BlockSpec(memory_space=pl.ANY)] * 2,
            scratch_shapes=scratch,
            compiler_params=pltpu.CompilerParams(
                collective_id=0, has_side_effects=True, vmem_limit_bytes=48 << 20
            ),
        )(forcing, surface_term, sea_cells, levels)

    return jax.shard_map(
        step,
        mesh=mesh,
        in_specs=(P("lat", "lon"),) * 4,
        out_specs=(P("lat", "lon"),) * 2,
        check_vma=False,
    )
```

time: 1200 us -> 42 us (0.04)
  blocking collectives: 806 us -> 0 us
  starting transfers between devices: 211 us -> 0 us
  waiting for transfers between devices: 119 us -> 0 us
  Pallas kernels: 0 us -> 36.5 us
  local copies, waits for them, and re-layouts: 22.1 us -> 4.61 us
  between operations: 17.5 us -> 0.65 us
  other arithmetic: 13.1 us -> 0 us
    psum x11 -> x0, blocking collectives: 806 us -> none  [grid_total(): return lax.psum(value, ('lon', 'lat'))]
    ppermute x92 -> x0, starting transfers between devices: 211 us -> none  [the longest x48 112 us: with_halo(): lax.ppermute(lax.slice_in_dim(block, block.shape[dim] - width, None, axis...]
    ppermute x92 -> x0, waiting for transfers between devices: 119 us -> none  [the longest x48 100 us: with_halo(): lax.ppermute(lax.slice_in_dim(block, block.shape[dim] - width, None, axis...]
    pallas_call x0 -> x1, Pallas kernels: none -> 36.5 us  [step(): pl.pallas_call(functools.partial(body, (lat_count, lon_count, ring)), out...]
    slice x93 -> x0, local copies, waits for them, and re-layouts: 17 us -> none  [the longest x45 2.06 us: with_halo(): lax.slice_in_dim(block, block.shape[dim] - width, None, axis=dim)]
  transfers between devices with their start and end apart: 92 -> 0, of which waited for: 59 -> 0; matrix products, arithmetic and copies ran while one was open for 1% -> 0% of each run, Pallas kernels for 0% -> 0%
where the time goes in v1:
time: 42 us; the launch traced here: 41.8 us
  Pallas kernels  36.5 us (87%)
  local copies, waits for them, and re-layouts  4.61 us (11%)
  between operations  0.65 us (2%)
    pallas_call x1, Pallas kernels, step(): pl.pallas_call(functools.partial(body, (lat_count, lon_count, ring)), out...  36.5 us
    unnamed x10, local copies, waits for them, and re-layouts  4.61 us

profile of v1, /device:TPU:1, one launch (start us, length us, event | category | flops | bytes accessed | tf_op | source)
XLA Modules:
  0.0 41.8 jit_solution(8716831562829346255)
XLA Ops:
  0.6 0.0 copy-start
  0.6 0.8 %copy-done = f32[64,256]{1,0:T(8,128)S(1)} copy-done((f32[64,256]{1,0:T(8,128)S(1)}, f32[64,256]{1,0:T(8,128)}, u32[]{:S(2)}) %copy-start) | copy-done | bytes 65560
  1.5 0.0 copy-start.1
  1.5 0.8 %copy-done.1 = f32[64,256]{1,0:T(8,128)S(1)} copy-done((f32[64,256]{1,0:T(8,128)S(1)}, f32[64,256]{1,0:T(8,128)}, u32[]{:S(2)}) %copy-start.1) | copy-done | bytes 65560
  2.3 0.0 copy-start.2
  2.3 0.8 %copy-done.2 = s32[64,256]{1,0:T(8,128)S(1)} copy-done((s32[64,256]{1,0:T(8,128)S(1)}, s32[64,256]{1,0:T(8,128)}, u32[]{:S(2)}) %copy-start.2) | copy-done | bytes 65560
  3.2 0.0 copy-start.3
  3.2 0.8 %copy-done.3 = s32[64,256]{1,0:T(8,128)S(1)} copy-done((s32[64,256]{1,0:T(8,128)S(1)}, s32[64,256]{1,0:T(8,128)}, u32[]{:S(2)}) %copy-start.3) | copy-done | bytes 65560
  4.0 36.5 %shard_map.59 = (f32[64,256]{1,0:T(8,128)S(1)}, f32[64,256]{1,0:T(8,128)S(1)}) custom-call(f32[64,256]{1,0:T(8,128)S(1)} %copy-done, f32[64,256]{1,0:T(8,128)S(1)} %copy-done.1, s32[64,256]{1,0:T(8,128)S(1)} %copy-done.2, s32[64,256]{1,0:T(8,128)S(1)} %copy-done.3), custom_call_target="tpu_custom_call" | custom-call | tf_op jit(solution)/shard_map/pallas_call | solution.py:608
  40.5 0.6 %copy.8 = f32[64,256]{1,0:T(8,128)} copy(f32[64,256]{1,0:T(8,128)S(1)} %get-tuple-element.4) | data formatting | bytes 131072
  41.1 0.6 %copy.9 = f32[64,256]{1,0:T(8,128)} copy(f32[64,256]{1,0:T(8,128)S(1)} %get-tuple-element.5) | data formatting | bytes 131072
Async XLA Ops:
  0.6 0.8 %copy-start = (f32[64,256]{1,0:T(8,128)S(1)}, f32[64,256]{1,0:T(8,128)}, u32[]{:S(2)}) copy-start(f32[64,256]{1,0:T(8,128)} %forcing.1) | copy-start | bytes 196612
  1.5 0.8 %copy-start.1 = (f32[64,256]{1,0:T(8,128)S(1)}, f32[64,256]{1,0:T(8,128)}, u32[]{:S(2)}) copy-start(f32[64,256]{1,0:T(8,128)} %surface.1) | copy-start | bytes 196612
  2.3 0.8 %copy-start.2 = (s32[64,256]{1,0:T(8,128)S(1)}, s32[64,256]{1,0:T(8,128)}, u32[]{:S(2)}) copy-start(s32[64,256]{1,0:T(8,128)} %sea.1) | copy-start | bytes 196612
  3.2 0.8 %copy-start.3 = (s32[64,256]{1,0:T(8,128)S(1)}, s32[64,256]{1,0:T(8,128)}, u32[]{:S(2)}) copy-start(s32[64,256]{1,0:T(8,128)} %depth_levels.1) | copy-start | bytes 196612

commit v2 on v1

--- a/solution.py
+++ b/solution.py
@@ -177,10 +177,11 @@
     ) = rest[27:]
     planes_y = lon_count // ring
     planes_x = lat_count // CORES
+    tiles = lon_count * (COLS >> 3) // LANES
+    per_line = tiles // planes_y
     la, lo = lax.axis_index("lat"), lax.axis_index("lon")
     x, core = la // CORES, la % CORES
     y, z = lo // ring, lo % ring
-    tiles = lon_count * (COLS >> 3) // LANES
     own_rows = ROWS >> 3
     group = LANES // (COLS >> 3)
 
@@ -207,8 +208,9 @@
     rims = [(dy, dx) for dy in (-1, 0, 1) for dx in (-1, 0, 1) if (dy, dx) != (0, 0)]
     hops = sorted(
         ((dx, dy) for dx in range(planes_x) for dy in range(planes_y) if (dx, dy) != (0, 0)),
-        key=lambda d: min(d[0], planes_x - d[0]) + min(d[1], planes_y - d[1]),
+        key=lambda d: -min(d[0], planes_x - d[0]) - min(d[1], planes_y - d[1]),
     )
+    ring_steps = sorted(range(1, ring), key=lambda d: -min(d, ring - d))
     barrier = pltpu.get_barrier_semaphore()
 
     def greet(lat, lon):
@@ -234,7 +236,7 @@
 
     for dy, dx in rims:
         where_inside(dy, lambda dy=dy, dx=dx: greet(*beside(dy, dx)))
-    for step in range(1, ring):
+    for step in ring_steps:
         greet(*ring_peer(step))
     for dx, dy in hops:
         greet(*plane_peer(dx, dy))
@@ -253,8 +255,8 @@
             for c in range(3):
                 clear(ref, c, 0, PAD)
                 clear(ref, c, PAD + level.rows, PAD)
-    for ref in (faces.at[1], rhs, bottom.at[0]):
-        for t in range(tiles):
+    for ref, count in ((faces.at[1], tiles), (rhs, tiles + planes_y), (bottom.at[0], tiles)):
+        for t in range(count):
             clear(ref, t, 0, PAD)
             clear(ref, t, PAD + lat_count * own_rows, PAD)
     for dy, row in ((-1, 0), (1, RIM + ROWS)):
@@ -299,6 +301,42 @@
         west_pack[own, :] = packed_west
         east_pack[own, :] = packed_east
 
+    own3 = RIM >> 3
+    lane = lane_of(own_rows)
+    line_row = lax.broadcasted_iota(jnp.int32, (own_rows, LANES), 0)
+    pick = (lane % 16) * 8
+    low = (lane % 32) < 16
+
+    def dense(west_tile, east_tile, last=0):
+        return jnp.where(
+            low, jnp.take_along_axis(west_tile, pick + last, axis=1), jnp.take_along_axis(east_tile, pick + last, axis=1)
+        )
+
+    def lane_sum(value):
+        for shift in (1, 2, 4):
+            value = pair_sum(value, shift, lane)
+        return value
+
+    def every8(k, c, row):
+        return fields[k, c, pl.ds(PAD + RIM + row, own_rows, stride=8), :]
+
+    sums = [[None, None] for _ in range(3)]
+    for row in range(8):
+        deep = [every8(0, c, row) for c in range(2)]
+        east = east_of(deep, 1, lane)
+        inverse = 1.0 / metric[0, pl.ds(RIM + row, own_rows, stride=8), :]
+        for c in range(2):
+            face, term = jnp.minimum(deep[c], east[c]) * inverse, every8(2, c, row)
+            sums[0][c] = face if row == 0 else sums[0][c] + face
+            sums[2][c] = term if row == 0 else sums[2][c] + term
+    for c in range(2):
+        above = pltpu.roll(every8(0, c, 0), own_rows - 1, 0)
+        face = jnp.minimum(every8(0, c, 7), above) * metric[1, pl.ds(RIM + 7, own_rows, stride=8), :]
+        sums[1][c] = lane_sum(face)
+        sums[2][c] = lane_sum(sums[2][c])
+    parts = [dense(*sums[0], last=7), dense(*sums[1]), dense(*sums[2])]
+    face_slots[z] = jnp.where(lane < 32, parts[0], jnp.where(lane < 64, parts[1], parts[2]))
+
     greeted = 2 + (ring - 1) + len(hops) + 1
     both = inside[-1].astype(jnp.int32) + inside[1].astype(jnp.int32)
     pl.semaphore_wait(barrier, greeted + 3 * both)
@@ -318,20 +356,77 @@
             device_id=device(*beside(dy, dx)), device_id_type=MESH,
         )
 
+    def slot_copy(slots, which, step):
+        return pltpu.make_async_remote_copy(
+            slots.at[z], slots.at[z], slot_send.at[which], slot_recv.at[which],
+            device_id=device(*ring_peer(step)), device_id_type=MESH,
+        )
+
+    def all_slots(slots, which):
+        return pltpu.make_async_remote_copy(
+            slots.at[pl.ds(0, ring - 1)], slots.at[pl.ds(0, ring - 1)], slot_send.at[which], slot_recv.at[which],
+            device_id=device(*ring_peer(1)), device_id_type=MESH,
+        )
+
+    def plane_block(which, lat, line):
+        rows = pl.ds(pl.multiple_of(PAD + lat * own_rows, 8), own_rows)
+        if which == 0:
+            return faces.at[:, pl.ds(line * per_line, per_line), rows, :]
+        return rhs.at[pl.ds(line * (per_line + 1), per_line + 1), rows, :]
+
+    def plane_copy(which, k, dx, dy):
+        block = plane_block(which, la, y)
+        return pltpu.make_async_remote_copy(
+            block, block, plane_send.at[which, k], plane_recv.at[which, k],
+            device_id=device(*plane_peer(dx, dy)), device_id_type=MESH,
+        )
+
+    def pass_copy(which, lat, line):
+        block = plane_block(which, lat, line)
+        return pltpu.make_async_remote_copy(
+            block, block, pass_send.at[which], pass_recv.at[which],
+            device_id=device(*partner), device_id_type=MESH,
+        )
+
+    def all_passed(which):
+        half = pl.ds(PAD, lat_count * own_rows // CORES)
+        block = faces.at[:, :, half, :] if which == 0 else rhs.at[:, half, :]
+        return pltpu.make_async_remote_copy(
+            block, block, pass_send.at[which], pass_recv.at[which],
+            device_id=device(*partner), device_id_type=MESH,
+        )
+
+    def send_plane(which):
+        for k, (dx, dy) in enumerate(hops):
+            plane_copy(which, k, dx, dy).start()
+        pass_copy(which, la, y).start()
+
+    def sent(which):
+        for k, (dx, dy) in enumerate(hops):
+            plane_copy(which, k, dx, dy).wait_send()
+        all_passed(which).wait_send()
+
+    def take_plane(which):
+        for k, (dx, dy) in reversed([*enumerate(hops)]):
+            plane_copy(which, k, dx, dy).wait_recv()
+            pass_copy(which, *(lax.rem(x - dx + planes_x, planes_x) * CORES + core, lax.rem(y - dy + planes_y, planes_y))).start()
+
     order = sorted(rims, key=lambda d: (d[1] == 0, d[0] == 0))
     for dy, dx in order:
         where_inside(dy, lambda dy=dy, dx=dx: rim_copy(dy, dx).start())
+    for step in ring_steps:
+        slot_copy(face_slots, 0, step).start()
     for dy, dx in order:
         where_inside(-dy, lambda dy=dy, dx=dx: rim_copy(dy, dx).wait_recv())
 
     for row in range(0, ROWS + 2 * RIM, CHUNK):
-        lane = lane_of(CHUNK)
+        wide_lane = lane_of(CHUNK)
         east, west = east_rim[pl.ds(row, CHUNK), :], west_rim[pl.ds(row, CHUNK), :]
         for k in range(3):
             moved_east = pltpu.roll(east, LANES - RIM * k, 1) if k else east
             moved_west = pltpu.roll(west, RIM * k, 1) if k else west
             fields[k, 2, pl.ds(PAD + row, CHUNK), :] = jnp.where(
-                lane < RIM, moved_east, jnp.where(lane >= LANES - RIM, moved_west, 0.0)
+                wide_lane < RIM, moved_east, jnp.where(wide_lane >= LANES - RIM, moved_west, 0.0)
             )
 
     top = levels[0]
@@ -351,91 +446,8 @@
                 at = pl.ds(PAD + row, coarse.chunk)
                 coarse.east[c, at, :], coarse.north[c, at, :], coarse.source[c, at, :] = fine.coarse_faces(c, row, coarse.chunk)
 
-    lane = lane_of(own_rows)
-    pick = (lane % 16) * 8
-    low = (lane % 32) < 16
-
-    def dense(west_tile, east_tile):
-        return jnp.where(
-            low, jnp.take_along_axis(west_tile, pick, axis=1), jnp.take_along_axis(east_tile, pick, axis=1)
-        )
-
-    own3 = RIM >> 3
-    bottom_faces = [levels[2].coarse_faces(c, own3, own_rows) for c in range(2)]
-    parts = [dense(bottom_faces[0][k], bottom_faces[1][k]) for k in range(3)]
-    face_slots[z] = jnp.where(lane < 32, parts[0], jnp.where(lane < 64, parts[1], parts[2]))
-
-    def slot_copy(slots, which, step):
-        return pltpu.make_async_remote_copy(
-            slots.at[z], slots.at[z], slot_send.at[which], slot_recv.at[which],
-            device_id=device(*ring_peer(step)), device_id_type=MESH,
-        )
-
-    def all_slots(slots, which):
-        return pltpu.make_async_remote_copy(
-            slots.at[pl.ds(0, ring - 1)], slots.at[pl.ds(0, ring - 1)], slot_send.at[which], slot_recv.at[which],
-            device_id=device(*ring_peer(1)), device_id_type=MESH,
-        )
-
-    def plane_block(which, lat, line):
-        rows = pl.ds(pl.multiple_of(PAD + lat * own_rows, 8), own_rows)
-        per_line = tiles // planes_y
-        if which == 0:
-            return faces.at[:, pl.ds(line * per_line, per_line), rows, :]
-        return rhs.at[pl.ds(line * per_line, per_line), rows, :]
-
-    def plane_copy(which, k, dx, dy):
-        block = plane_block(which, la, y)
-        return pltpu.make_async_remote_copy(
-            block, block, plane_send.at[which, k], plane_recv.at[which, k],
-            device_id=device(*plane_peer(dx, dy)), device_id_type=MESH,
-        )
-
-    def pass_copy(which, lat, line):
-        block = plane_block(which, lat, line)
-        return pltpu.make_async_remote_copy(
-            block, block, pass_send.at[which], pass_recv.at[which],
-            device_id=device(*partner), device_id_type=MESH,
-        )
-
-    def all_passed(which):
-        half = pl.ds(PAD, lat_count * own_rows // CORES)
-        block = faces.at[:, :, half, :] if which == 0 else rhs.at[:, half, :]
-        return pltpu.make_async_remote_copy(
-            block, block, pass_send.at[which], pass_recv.at[which],
-            device_id=device(*partner), device_id_type=MESH,
-        )
-
-    def send_plane(which):
-        for k, (dx, dy) in enumerate(hops):
-            plane_copy(which, k, dx, dy).start()
-        pass_copy(which, la, y).start()
-
-    def take_plane(which):
-        for k, (dx, dy) in enumerate(hops):
-            plane_copy(which, k, dx, dy).wait_recv()
-            pass_copy(which, *(lax.rem(x - dx + planes_x, planes_x) * CORES + core, lax.rem(y - dy + planes_y, planes_y))).start()
-
-    for step in range(1, ring):
-        slot_copy(face_slots, 0, step).start()
-
     levels[0].finish()
     levels[0].descend()
-
-    all_slots(face_slots, 0).wait_recv()
-    per_line = tiles // planes_y
-    own_at = pl.ds(pl.multiple_of(PAD + la * own_rows, 8), own_rows)
-    for h in range(per_line):
-        for k in range(3):
-            value = None
-            for j in range(group):
-                slot = face_slots[h * group + j]
-                shift = (32 * (j - k)) % LANES
-                moved = pltpu.roll(slot, shift, 1) if shift else slot
-                value = moved if value is None else jnp.where(lane // 32 == j, moved, value)
-            faces[k, y * per_line + h, own_at, :] = value
-    send_plane(0)
-
     for fine, coarse in zip(levels, levels[1:]):
         for row in coarse.chunks():
             for c in range(3):
@@ -443,17 +455,43 @@
         coarse.finish()
         coarse.descend()
 
+    bottom_faces = [levels[2].coarse_faces(c, own3, own_rows) for c in range(2)]
     bottom_rhs = [levels[2].coarse_rhs(c, own3, own_rows) for c in range(2)]
-    rhs_slots[z] = dense(*bottom_rhs)
-    for step in range(1, ring):
+    last = jnp.take_along_axis(bottom_faces[1][0], jnp.full_like(lane, LANES - 1), axis=1)
+    last = jnp.where(lane % 8 == line_row, last, 0.0)
+    for shift in (4, 2, 1):
+        last = last + pltpu.roll(last, shift, 0)
+    rhs_slots[z] = jnp.where(
+        lane < 32, dense(*bottom_rhs), jnp.where(lane < 64, dense(bottom_faces[0][1], bottom_faces[1][1]), last)
+    )
+    for step in ring_steps:
         slot_copy(rhs_slots, 1, step).start()
-    all_slots(rhs_slots, 1).wait_recv()
-    for h in range(per_line):
+
+    def gathered(slots, h, k):
         value = None
         for j in range(group):
-            slot = rhs_slots[h * group + j]
-            value = slot if value is None else jnp.where(lane // 32 == j, slot, value)
-        rhs[y * per_line + h, own_at, :] = value
+            slot = slots[h * group + j]
+            shift = (32 * (j - k)) % LANES
+            moved = pltpu.roll(slot, shift, 1) if shift else slot
+            value = moved if value is None else jnp.where(lane // 32 == j, moved, value)
+        return value
+
+    own_at = pl.ds(pl.multiple_of(PAD + la * own_rows, 8), own_rows)
+    all_slots(face_slots, 0).wait_recv()
+    for h in range(per_line):
+        for k in range(3):
+            faces[k, y * per_line + h, own_at, :] = gathered(face_slots, h, k)
+    send_plane(0)
+    all_slots(rhs_slots, 1).wait_recv()
+    edge = None
+    for j in range(ring):
+        moved = pltpu.roll(rhs_slots[j], LANES // 2, 1) if 8 * j < LANES // 2 else rhs_slots[j]
+        edge = moved if edge is None else jnp.where(lane // 8 == j, moved, edge)
+    for h in range(per_line):
+        rhs[y * (per_line + 1) + h, own_at, :] = gathered(rhs_slots, h, 0)
+        north = gathered(rhs_slots, h, 1)
+        edge = jnp.where(line_row == 7 - h, pltpu.roll(north, 8 - h, 0) if h else north, edge)
+    rhs[y * (per_line + 1) + per_line, own_at, :] = edge
     send_plane(1)
     take_plane(0)
     take_plane(1)
@@ -464,6 +502,22 @@
     west_face, diagonal = bottom.at[1], bottom.at[2]
     rest_ref, image_ref, along_ref = bottom.at[0], bottom.at[3], bottom.at[4]
     all_passed(0).wait_recv()
+    all_passed(1).wait_recv()
+
+    def rhs_tile(t):
+        return t // per_line * (per_line + 1) + t % per_line
+
+    sent(0)
+    lane_lat = lane_of(lat_count)
+    for t in range(tiles):
+        h, edge_tile = t % per_line, t // per_line * (per_line + 1) + per_line
+        side = pl.ds(PAD + 7, lat_count, stride=8)
+        faces[1, t, side, :] = rhs[edge_tile, pl.ds(PAD + 7 - h, lat_count, stride=8), :]
+        east = rhs[edge_tile, pl.ds(PAD, lat_count, stride=8), :]
+        for row in range(own_rows):
+            at = pl.ds(PAD + row, lat_count, stride=8)
+            moved = jnp.take_along_axis(east, 8 * (h * group + lane_lat // 32) + row, axis=1)
+            faces[0, t, at, :] = jnp.where(lane_lat % 32 == 31, moved, faces[0, t, at, :])
     for t in range(tiles):
         east = faces[0, t, everything, :]
         before = faces[0, (t - 1) % tiles, everything, :]
@@ -473,19 +527,18 @@
             faces[2, t, everything, :] + east + west
             + faces[1, t, everything, :] + faces[1, t, pl.ds(PAD - 1, height), :]
         )
-    all_passed(1).wait_recv()
-
-    def operate(ref):
+
+    def operate(ref, place):
         norm, product = None, None
         for t in range(tiles):
-            value = ref[t, everything, :]
-            east = pltpu.roll(jnp.where(lane3 < 1, ref[(t + 1) % tiles, everything, :], value), LANES - 1, 1)
-            west = pltpu.roll(jnp.where(lane3 >= LANES - 1, ref[(t - 1) % tiles, everything, :], value), 1, 1)
+            value = ref[place(t), everything, :]
+            east = pltpu.roll(jnp.where(lane3 < 1, ref[place((t + 1) % tiles), everything, :], value), LANES - 1, 1)
+            west = pltpu.roll(jnp.where(lane3 >= LANES - 1, ref[place((t - 1) % tiles), everything, :], value), 1, 1)
             image = diagonal[t, everything, :] * value - (
                 faces[0, t, everything, :] * east
                 + west_face[t, everything, :] * west
-                + faces[1, t, everything, :] * ref[t, pl.ds(PAD + 1, height), :]
-                + faces[1, t, pl.ds(PAD - 1, height), :] * ref[t, pl.ds(PAD - 1, height), :]
+                + faces[1, t, everything, :] * ref[place(t), pl.ds(PAD + 1, height), :]
+                + faces[1, t, pl.ds(PAD - 1, height), :] * ref[place(t), pl.ds(PAD - 1, height), :]
             )
             image_ref[t, everything, :] = image
             square, mixed = value * value, value * image
@@ -498,13 +551,13 @@
     near = pl.ds(pl.multiple_of(la * own_rows, 8), 2 * PAD + own_rows)
     solved = [None] * 3
     direction = [None] * 3
-    norm, product = operate(rhs)
+    norm, product = operate(rhs, rhs_tile)
     alpha = norm / product
     beta = None
     for iteration in range(BOTTOM_ITERS):
-        current = rhs if iteration == 0 else rest_ref
+        current, tile_at = (rhs, rhs_tile) if iteration == 0 else (rest_ref, lambda t: t)
         for k in range(3):
-            value = current[near_tiles[k], near, :]
+            value = current[tile_at(near_tiles[k]), near, :]
             direction[k] = value if iteration == 0 else value + beta * direction[k]
             solved[k] = alpha * direction[k] if iteration == 0 else solved[k] + alpha * direction[k]
         if iteration == BOTTOM_ITERS - 1:
@@ -514,8 +567,8 @@
             if iteration:
                 along = along + beta * along_ref[t, everything, :]
             along_ref[t, everything, :] = along
-            rest_ref[t, everything, :] = current[t, everything, :] - alpha * along
-        norm_next, product = operate(rest_ref)
+            rest_ref[t, everything, :] = current[tile_at(t), everything, :] - alpha * along
+        norm_next, product = operate(rest_ref, lambda t: t)
         beta = norm_next / norm
         alpha = norm_next / (product - beta * norm_next / alpha)
         norm = norm_next
@@ -554,11 +607,20 @@
         where_inside(dy, lambda dy=dy, dx=dx: rim_copy(dy, dx).wait_send())
     for which, slots in enumerate((face_slots, rhs_slots)):
         all_slots(slots, which).wait_send()
-        for k, (dx, dy) in enumerate(hops):
-            plane_copy(which, k, dx, dy).wait_send()
-        all_passed(which).wait_send()
+    sent(1)
     for store in stores:
         store.wait()
+
+
+def put_out(solution_in, residual_in, solution_out, residual_out, sems):
+    copies = [
+        pltpu.make_async_copy(solution_in, solution_out, sems.at[0]),
+        pltpu.make_async_copy(residual_in, residual_out, sems.at[1]),
+    ]
+    for copy in copies:
+        copy.start()
+    for copy in copies:
+        copy.wait()
 
 
 def solution(mesh, ring=RING):
@@ -587,7 +649,7 @@
         pltpu.VMEM((ring, 8, LANES), f32),
         pltpu.VMEM((ring, 8, LANES), f32),
         pltpu.VMEM((3, tiles, height, LANES), f32),
-        pltpu.VMEM((tiles, height, LANES), f32),
+        pltpu.VMEM((tiles + lon_count // ring, height, LANES), f32),
         pltpu.VMEM((5, tiles, height, LANES), f32),
         padded(0),
         pltpu.VMEM((3, 2 * PAD + (ROWS >> 3), LANES), f32),
@@ -605,16 +667,23 @@
 
     def step(forcing, surface_term, sea_cells, levels):
         out = jax.ShapeDtypeStruct(forcing.shape, f32)
-        return pl.pallas_call(
+        results = pl.pallas_call(
             functools.partial(body, (lat_count, lon_count, ring)),
             out_shape=(out, out),
-            in_specs=[pl.BlockSpec(memory_space=pl.ANY)] * 4,
+            in_specs=[pl.BlockSpec(memory_space=pltpu.HBM)] * 4,
             out_specs=[pl.BlockSpec(memory_space=pl.ANY)] * 2,
             scratch_shapes=scratch,
             compiler_params=pltpu.CompilerParams(
                 collective_id=0, has_side_effects=True, vmem_limit_bytes=48 << 20
             ),
-        )(forcing, surface_term, sea_cells, levels)
+        )(*(pltpu.with_memory_space_constraint(v, pltpu.HBM) for v in (forcing, surface_term, sea_cells, levels)))
+        return pl.pallas_call(
+            put_out,
+            out_shape=(out, out),
+            in_specs=[pl.BlockSpec(memory_space=pltpu.VMEM)] * 2,
+            out_specs=[pl.BlockSpec(memory_space=pltpu.HBM)] * 2,
+            scratch_shapes=[pltpu.SemaphoreType.DMA((2,))],
+        )(*(pltpu.with_memory_space_constraint(v, pltpu.VMEM) for v in results))
 
     return jax.shard_map(
         step,

time: 42 us -> 33.4 us (0.80)
  local copies, waits for them, and re-layouts: 4.61 us -> 0 us
  Pallas kernels: 36.5 us -> 32.6 us
    unnamed x10 -> x0, local copies, waits for them, and re-layouts: 4.61 us -> none
    pallas_call x1, Pallas kernels: 36.5 us -> 31.9 us  [step(): pl.pallas_call(functools.partial(body, (lat_count, lon_count, ring)), out...]
    pallas_call x0 -> x1, Pallas kernels: none -> 0.67 us  [step(): pl.pallas_call(put_out, out_shape=(out, out), in_specs=[pl.BlockSpec(memo...]
where the time goes in v2:
time: 33.4 us; the launch traced here: 33.2 us
  Pallas kernels  32.6 us (98%)
  between operations  0.64 us (2%)
    pallas_call x1, Pallas kernels, step(): pl.pallas_call(functools.partial(body, (lat_count, lon_count, ring)), out...  31.9 us
    pallas_call x1, Pallas kernels, step(): pl.pallas_call(put_out, out_shape=(out, out), in_specs=[pl.BlockSpec(memo...  0.67 us

profile of v2, /device:TPU:1, one launch (start us, length us, event | category | flops | bytes accessed | tf_op | source)
XLA Modules:
  0.0 33.2 jit_solution(1811322967380026603)
XLA Ops:
  0.6 31.9 %shard_map.59 = (f32[64,256]{1,0:T(8,128)S(1)}, f32[64,256]{1,0:T(8,128)S(1)}) custom-call(f32[64,256]{1,0:T(8,128)} %forcing.1, f32[64,256]{1,0:T(8,128)} %surface.1, s32[64,256]{1,0:T(8,128)} %sea.1, s32[64,256]{1,0:T(8,128)} %depth_levels.1), custom_call_target="tpu_custom_call" | custom-call | tf_op jit(solution)/shard_map/pallas_call | solution.py:670
  32.6 0.7 %shard_map.60 = (f32[64,256]{1,0:T(8,128)}, f32[64,256]{1,0:T(8,128)}) custom-call(f32[64,256]{1,0:T(8,128)S(1)} %get-tuple-element.4.solution_in, f32[64,256]{1,0:T(8,128)S(1)} %get-tuple-element.5.residual_in), custom_call_target="tpu_custom_call" | custom-call | tf_op jit(solution)/shard_map/pallas_call | solution.py:680

commit v3 on v2

--- a/solution.py
+++ b/solution.py
@@ -19,6 +19,7 @@
 
 ROWS, COLS = 64, 256
 RIM = 32
+NEAR = 16
 PAD = 8
 LANES = 128
 CHUNK = 32
@@ -63,13 +64,13 @@
 
 
 class Level:
-    def __init__(self, index, refs):
+    def __init__(self, index, rim, refs):
         self.index = index
         self.shift = 1 << index
-        self.rows = (ROWS + 2 * RIM) >> index
-        self.rim = RIM >> index
+        self.rows = (ROWS + 2 * rim) >> index
+        self.rim = rim >> index
         self.east, self.west, self.north, self.source, self.diag, self.scale, self.rhs, self.va, self.vb, self.tmp = refs
-        self.chunk = min(CHUNK, self.rows)
+        self.chunk = next(n for n in (32, 24, 16, 8) if self.rows % n == 0)
 
     def chunks(self):
         return range(0, self.rows, self.chunk)
@@ -168,13 +169,14 @@
     in_f, in_i, fields, *rest
 ):
     lat_count, lon_count, ring = shape
-    level_refs = [rest[0:7], rest[7:17], rest[17:27]]
+    level_refs = [rest[0:8], rest[8:18], rest[18:28]]
+    near_fields, near_refs = rest[28], [rest[29:37], rest[37:47], rest[47:57]]
     (
-        west_pack, east_pack, east_rim, west_rim, metric,
-        face_slots, rhs_slots, faces, rhs, bottom, wide, piece,
+        west_pack, east_pack, east_rim, west_rim, near_packs, near_rims, near_corners, metric,
+        face_slots, rhs_slots, side_slots, faces, rhs, sides, bottom, piece,
         in_sem, out_sem, rim_send, rim_recv, slot_send, slot_recv,
-        plane_send, plane_recv, pass_send, pass_recv,
-    ) = rest[27:]
+        plane_send, bulk_recv, plane_recv, pass_send, pass_recv,
+    ) = rest[57:]
     planes_y = lon_count // ring
     planes_x = lat_count // CORES
     tiles = lon_count * (COLS >> 3) // LANES
@@ -185,12 +187,13 @@
     own_rows = ROWS >> 3
     group = LANES // (COLS >> 3)
 
-    depth = fields.at[0]
-    levels = [
-        Level(0, (*level_refs[0][0:3], fields.at[2], *level_refs[0][3:5], fields.at[1], *level_refs[0][5:7], wide)),
-        Level(1, level_refs[1]),
-        Level(2, level_refs[2]),
-    ]
+    def levels_of(rim, base, refs):
+        first = (*refs[0][0:3], base.at[2], *refs[0][3:5], base.at[1], *refs[0][5:8])
+        return [Level(0, rim, first), Level(1, rim, refs[1]), Level(2, rim, refs[2])]
+
+    levels = levels_of(RIM, fields, level_refs)
+    near_levels = levels_of(NEAR, near_fields, near_refs)
+    top = levels[0]
 
     def device(lat, lon):
         return {"lat": lat, "lon": lon}
@@ -245,27 +248,29 @@
     def clear(ref, col, row, count):
         ref[col, pl.ds(row, count), :] = jnp.zeros((count, LANES), ref.dtype)
 
-    for k in range(3):
-        clear_to = fields.at[k]
+    for base, group_of in ((fields, levels), (near_fields, near_levels)):
         for c in range(3):
-            clear(clear_to, c, 0, PAD)
-            clear(clear_to, c, PAD + ROWS + 2 * RIM, PAD)
-    for level in levels:
-        for ref in (level.north, level.va, level.vb):
-            for c in range(3):
-                clear(ref, c, 0, PAD)
-                clear(ref, c, PAD + level.rows, PAD)
-    for ref, count in ((faces.at[1], tiles), (rhs, tiles + planes_y), (bottom.at[0], tiles)):
-        for t in range(count):
+            for k in range(3):
+                clear(base.at[k], c, 0, PAD)
+                clear(base.at[k], c, PAD + group_of[0].rows, PAD)
+            for level in group_of:
+                for ref in (level.north, level.va, level.vb):
+                    clear(ref, c, 0, PAD)
+                    clear(ref, c, PAD + level.rows, PAD)
+    for ref in (faces.at[1], rhs, bottom.at[0], bottom.at[6]):
+        for t in range(tiles):
             clear(ref, t, 0, PAD)
             clear(ref, t, PAD + lat_count * own_rows, PAD)
-    for dy, row in ((-1, 0), (1, RIM + ROWS)):
+    for dy, row, near_row in ((-1, 0, 0), (1, RIM + ROWS, NEAR + ROWS)):
 
         @pl.when(jnp.logical_not(inside[dy]))
-        def _(row=row):
+        def _(dy=dy, row=row, near_row=near_row):
             for k in range(3):
                 for c in range(2):
                     clear(fields.at[k], c, PAD + row, RIM)
+                    clear(near_fields.at[k], c, PAD + near_row, NEAR)
+            for side in range(2):
+                clear(near_corners.at[side], (dy + 1) // 2, 0, NEAR)
             east_rim[pl.ds(row, RIM), :] = jnp.zeros((RIM, LANES), jnp.float32)
             west_rim[pl.ds(row, RIM), :] = jnp.zeros((RIM, LANES), jnp.float32)
 
@@ -277,6 +282,7 @@
 
     for load in loads:
         load.wait()
+    near_strips = [None, None]
     for row in range(0, ROWS, CHUNK):
         at = pl.ds(PAD + RIM + row, CHUNK)
         center = metric[0, pl.ds(RIM + row, CHUNK), :]
@@ -292,6 +298,7 @@
             values.append((deep, right, source))
             for k in range(3):
                 fields[k, c, at, :] = values[c][k]
+                near_fields[k, c, pl.ds(PAD + NEAR + row, CHUNK), :] = values[c][k]
         packed_west, packed_east = values[0][0], values[1][0]
         for k in range(1, 3):
             part = (lane >= RIM * k) & (lane < RIM * (k + 1))
@@ -300,6 +307,14 @@
             packed_east = jnp.where(part, pltpu.roll(values[1][k], LANES - RIM * k, 1), packed_east)
         west_pack[own, :] = packed_west
         east_pack[own, :] = packed_east
+        for side in range(2):
+            for k in range(3):
+                place = row * 2 + NEAR * k
+                moved = pltpu.roll(values[side][k], (place + NEAR * side) % LANES, 1)
+                part = (lane >= place) & (lane < place + NEAR)
+                near_strips[side] = moved if near_strips[side] is None else jnp.where(part, moved, near_strips[side])
+    for side in range(2):
+        near_packs[side] = near_strips[side]
 
     own3 = RIM >> 3
     lane = lane_of(own_rows)
@@ -341,20 +356,53 @@
     both = inside[-1].astype(jnp.int32) + inside[1].astype(jnp.int32)
     pl.semaphore_wait(barrier, greeted + 3 * both)
 
-    def rim_copy(dy, dx):
-        source_row, target_row = {1: (ROWS - RIM, 0), -1: (0, RIM + ROWS), 0: (0, RIM)}[dy]
-        count = ROWS if dy == 0 else RIM
-        if dx == 0:
-            source = fields.at[:, pl.ds(0, 2), pl.ds(PAD + RIM + source_row, count), :]
-            target = fields.at[:, pl.ds(0, 2), pl.ds(PAD + target_row, count), :]
-        else:
-            source = (east_pack if dx > 0 else west_pack).at[pl.ds(source_row, count), :]
-            target = (west_rim if dx > 0 else east_rim).at[pl.ds(target_row, count), :]
-        k = rims.index((dy, dx))
+    def to_beside(source, target, k, dy, dx):
         return pltpu.make_async_remote_copy(
             source, target, rim_send.at[k], rim_recv.at[k],
             device_id=device(*beside(dy, dx)), device_id_type=MESH,
         )
+
+    def rim_copy(dy, dx):
+        k = 1 if dx == 0 else 2
+        if dx == 0:
+            source_row, target_row = (ROWS - RIM, 0) if dy > 0 else (0, RIM + ROWS)
+            return to_beside(
+                fields.at[:, pl.ds(0, 2), pl.ds(PAD + RIM + source_row, RIM), :],
+                fields.at[:, pl.ds(0, 2), pl.ds(PAD + target_row, RIM), :], k, dy, dx,
+            )
+        source_row, target_row = {1: (ROWS - RIM, 0), -1: (0, RIM + ROWS), 0: (0, RIM)}[dy]
+        count = ROWS if dy == 0 else RIM
+        return to_beside(
+            (east_pack if dx > 0 else west_pack).at[pl.ds(source_row, count), :],
+            (west_rim if dx > 0 else east_rim).at[pl.ds(target_row, count), :], k, dy, dx,
+        )
+
+    def near_copy(dy, dx):
+        k = 0
+        if dx == 0:
+            source_row, target_row = (ROWS - NEAR, 0) if dy > 0 else (0, NEAR + ROWS)
+            return to_beside(
+                near_fields.at[:, pl.ds(0, 2), pl.ds(PAD + NEAR + source_row, NEAR), :],
+                near_fields.at[:, pl.ds(0, 2), pl.ds(PAD + target_row, NEAR), :], k, dy, dx,
+            )
+        side = (dx + 1) // 2
+        if dy == 0:
+            return to_beside(near_packs.at[side], near_rims.at[side], k, dy, dx)
+        source_row = NEAR if dy > 0 else 0
+        return to_beside(
+            near_packs.at[side, pl.ds(source_row, NEAR), :], near_corners.at[side, (1 - dy) // 2], k, dy, dx
+        )
+
+    def all_rims(k, wait):
+        per_side = ((6 + 2) * NEAR, 6 * RIM, 2 * RIM)[k]
+        level_with = (ROWS, 0, 2 * ROWS)[k]
+        between = jnp.logical_and(inside[-1], inside[1])
+        for when, count in ((between, 2 * per_side + level_with), (jnp.logical_not(between), per_side + level_with)):
+
+            @pl.when(when)
+            def _(count=count):
+                as_much = fields.at[pl.ds(0, 2), pl.ds(0, 2), pl.ds(0, count // 4), :]
+                wait(to_beside(as_much, as_much, k, 0, 1))
 
     def slot_copy(slots, which, step):
         return pltpu.make_async_remote_copy(
@@ -372,13 +420,25 @@
         rows = pl.ds(pl.multiple_of(PAD + lat * own_rows, 8), own_rows)
         if which == 0:
             return faces.at[:, pl.ds(line * per_line, per_line), rows, :]
-        return rhs.at[pl.ds(line * (per_line + 1), per_line + 1), rows, :]
+        if which == 1:
+            return rhs.at[pl.ds(line * per_line, per_line), rows, :]
+        return sides.at[line, rows, :]
 
     def plane_copy(which, k, dx, dy):
         block = plane_block(which, la, y)
         return pltpu.make_async_remote_copy(
-            block, block, plane_send.at[which, k], plane_recv.at[which, k],
+            block, block, plane_send.at[which], plane_recv.at[k] if which == 1 else bulk_recv.at[which // 2],
             device_id=device(*plane_peer(dx, dy)), device_id_type=MESH,
+        )
+
+    def all_planes(which):
+        count = len(hops)
+        lines, rows = (3, count // 3 * 8) if count % 3 == 0 else (1, count * 8)
+        rows, of_tiles = pl.ds(0, rows), pl.ds(0, lines * per_line)
+        block = (faces.at[:, of_tiles, rows, :], rhs.at[of_tiles, rows, :], sides.at[pl.ds(0, lines), rows, :])[which]
+        return pltpu.make_async_remote_copy(
+            block, block, plane_send.at[which], bulk_recv.at[which // 2],
+            device_id=device(*partner), device_id_type=MESH,
         )
 
     def pass_copy(which, lat, line):
@@ -390,7 +450,7 @@
 
     def all_passed(which):
         half = pl.ds(PAD, lat_count * own_rows // CORES)
-        block = faces.at[:, :, half, :] if which == 0 else rhs.at[:, half, :]
+        block = (faces.at[:, :, half, :], rhs.at[:, half, :], sides.at[:, half, :])[which]
         return pltpu.make_async_remote_copy(
             block, block, pass_send.at[which], pass_recv.at[which],
             device_id=device(*partner), device_id_type=MESH,
@@ -399,12 +459,22 @@
     def send_plane(which):
         for k, (dx, dy) in enumerate(hops):
             plane_copy(which, k, dx, dy).start()
-        pass_copy(which, la, y).start()
+        if which == 1:
+            pass_copy(which, la, y).start()
 
     def sent(which):
-        for k, (dx, dy) in enumerate(hops):
-            plane_copy(which, k, dx, dy).wait_send()
+        all_planes(which).wait_send()
         all_passed(which).wait_send()
+
+    def take_bulk(which):
+        all_planes(which).wait_recv()
+        for line in range(planes_x):
+            rows = pl.ds(pl.multiple_of(PAD + (line * CORES + core) * own_rows, 8), own_rows)
+            block = faces.at[:, :, rows, :] if which == 0 else sides.at[:, rows, :]
+            pltpu.make_async_remote_copy(
+                block, block, pass_send.at[which], pass_recv.at[which],
+                device_id=device(*partner), device_id_type=MESH,
+            ).start()
 
     def take_plane(which):
         for k, (dx, dy) in reversed([*enumerate(hops)]):
@@ -413,12 +483,98 @@
 
     order = sorted(rims, key=lambda d: (d[1] == 0, d[0] == 0))
     for dy, dx in order:
-        where_inside(dy, lambda dy=dy, dx=dx: rim_copy(dy, dx).start())
+        where_inside(dy, lambda dy=dy, dx=dx: near_copy(dy, dx).start())
     for step in ring_steps:
         slot_copy(face_slots, 0, step).start()
     for dy, dx in order:
-        where_inside(-dy, lambda dy=dy, dx=dx: rim_copy(dy, dx).wait_recv())
-
+        where_inside(dy, lambda dy=dy, dx=dx: rim_copy(dy, dx).start())
+
+    def find_faces(some, base):
+        first = some[0]
+        n = first.chunk
+        for row in first.chunks():
+            deep = [first.load(base.at[0], c, row, n) for c in range(3)]
+            east = east_of(deep, 1, lane_of(n))
+            inverse = 1.0 / metric[0, pl.ds(RIM - first.rim + row, n), :]
+            northern = metric[1, pl.ds(RIM - first.rim + row, n), :]
+            for c in range(3):
+                at = pl.ds(PAD + row, n)
+                first.east[c, at, :] = jnp.minimum(deep[c], east[c]) * inverse
+                first.north[c, at, :] = jnp.minimum(deep[c], first.load(base.at[0], c, row + 1, n)) * northern
+        for fine, coarse in zip(some, some[1:]):
+            for row in coarse.chunks():
+                for c in range(3):
+                    at = pl.ds(PAD + row, coarse.chunk)
+                    coarse.east[c, at, :], coarse.north[c, at, :], coarse.source[c, at, :] = fine.coarse_faces(c, row, coarse.chunk)
+
+    def descend(some):
+        some[0].finish()
+        some[0].descend()
+        for fine, coarse in zip(some, some[1:]):
+            for row in coarse.chunks():
+                for c in range(3):
+                    coarse.rhs[c, pl.ds(PAD + row, coarse.chunk), :] = fine.coarse_rhs(c, row, coarse.chunk)
+            coarse.finish()
+            coarse.descend()
+
+    all_rims(0, lambda copy: copy.wait_recv())
+
+    half_rows = ROWS // 2
+    for row, count, quarter in (
+        (0, NEAR, 1), (NEAR, half_rows, 0), (NEAR + half_rows, half_rows, 1), (NEAR + ROWS, NEAR, 0)
+    ):
+        wide_lane = lane_of(count)
+        if count == NEAR:
+            east, west = (near_corners[side, 0 if row == 0 else 1] for side in range(2))
+        else:
+            east, west = near_rims[0], near_rims[1]
+        for k in range(3):
+            place = quarter * (LANES // 2) + NEAR * k
+            moved_east = pltpu.roll(east, LANES - place, 1) if place else east
+            moved_west = pltpu.roll(west, LANES - NEAR - place, 1)
+            near_fields[k, 2, pl.ds(PAD + row, count), :] = jnp.where(
+                wide_lane < NEAR, moved_east, jnp.where(wide_lane >= LANES - NEAR, moved_west, 0.0)
+            )
+
+    find_faces(near_levels, near_fields)
+    near3 = NEAR >> 3
+    bottom_faces = [near_levels[2].coarse_faces(c, near3, own_rows) for c in range(2)]
+    last = jnp.take_along_axis(bottom_faces[1][0], jnp.full_like(lane, LANES - 1), axis=1)
+    last = jnp.where(lane % 8 == line_row, last, 0.0)
+    for shift in (4, 2, 1):
+        last = last + pltpu.roll(last, shift, 0)
+    north = pltpu.roll(dense(bottom_faces[0][1], bottom_faces[1][1]), 1, 0)
+    side_slots[z] = jnp.where(line_row == 0, north, last)[0:2]
+    for step in ring_steps:
+        slot_copy(side_slots, 2, step).start()
+    descend(near_levels)
+
+    bottom_rhs = [near_levels[2].coarse_rhs(c, near3, own_rows) for c in range(2)]
+    packed = jnp.where(lane // 32 == line_row // 2, dense(*bottom_rhs), 0.0)
+    for shift in (4, 2):
+        packed = packed + pltpu.roll(packed, shift, 0)
+    rhs_slots[z] = packed[0:2]
+    for step in ring_steps:
+        slot_copy(rhs_slots, 1, step).start()
+
+    own_at = pl.ds(pl.multiple_of(PAD + la * own_rows, 8), own_rows)
+    all_slots(face_slots, 0).wait_recv()
+    for h in range(per_line):
+        for k in range(3):
+            value = None
+            for j in range(group):
+                slot = face_slots[h * group + j]
+                shift = (32 * (j - k)) % LANES
+                moved = pltpu.roll(slot, shift, 1) if shift else slot
+                value = moved if value is None else jnp.where(lane // 32 == j, moved, value)
+            faces[k, y * per_line + h, own_at, :] = value
+    send_plane(0)
+
+    def spread(ref, j, row):
+        return jnp.broadcast_to(ref[j, pl.ds(row, 1), :], (own_rows, LANES))
+
+    for k in (1, 2):
+        all_rims(k, lambda copy: copy.wait_recv())
     for row in range(0, ROWS + 2 * RIM, CHUNK):
         wide_lane = lane_of(CHUNK)
         east, west = east_rim[pl.ds(row, CHUNK), :], west_rim[pl.ds(row, CHUNK), :]
@@ -428,72 +584,32 @@
             fields[k, 2, pl.ds(PAD + row, CHUNK), :] = jnp.where(
                 wide_lane < RIM, moved_east, jnp.where(wide_lane >= LANES - RIM, moved_west, 0.0)
             )
-
-    top = levels[0]
-    for row in top.chunks():
-        n = top.chunk
-        deep = [top.load(depth, c, row, n) for c in range(3)]
-        east = east_of(deep, 1, lane_of(n))
-        inverse = 1.0 / metric[0, pl.ds(row, n), :]
-        northern = metric[1, pl.ds(row, n), :]
-        for c in range(3):
-            at = pl.ds(PAD + row, n)
-            top.east[c, at, :] = jnp.minimum(deep[c], east[c]) * inverse
-            top.north[c, at, :] = jnp.minimum(deep[c], top.load(depth, c, row + 1, n)) * northern
-    for fine, coarse in zip(levels, levels[1:]):
-        for row in coarse.chunks():
-            for c in range(3):
-                at = pl.ds(PAD + row, coarse.chunk)
-                coarse.east[c, at, :], coarse.north[c, at, :], coarse.source[c, at, :] = fine.coarse_faces(c, row, coarse.chunk)
-
-    levels[0].finish()
-    levels[0].descend()
-    for fine, coarse in zip(levels, levels[1:]):
-        for row in coarse.chunks():
-            for c in range(3):
-                coarse.rhs[c, pl.ds(PAD + row, coarse.chunk), :] = fine.coarse_rhs(c, row, coarse.chunk)
-        coarse.finish()
-        coarse.descend()
-
-    bottom_faces = [levels[2].coarse_faces(c, own3, own_rows) for c in range(2)]
-    bottom_rhs = [levels[2].coarse_rhs(c, own3, own_rows) for c in range(2)]
-    last = jnp.take_along_axis(bottom_faces[1][0], jnp.full_like(lane, LANES - 1), axis=1)
-    last = jnp.where(lane % 8 == line_row, last, 0.0)
-    for shift in (4, 2, 1):
-        last = last + pltpu.roll(last, shift, 0)
-    rhs_slots[z] = jnp.where(
-        lane < 32, dense(*bottom_rhs), jnp.where(lane < 64, dense(bottom_faces[0][1], bottom_faces[1][1]), last)
-    )
-    for step in ring_steps:
-        slot_copy(rhs_slots, 1, step).start()
-
-    def gathered(slots, h, k):
+    find_faces(levels, fields)
+    descend(levels)
+
+    all_slots(side_slots, 2).wait_recv()
+    side = None
+    for j in range(ring):
+        value = spread(side_slots, j, 1)
+        side = value if side is None else jnp.where(lane // 8 == j, value, side)
+    for h in range(per_line):
+        for j in range(group):
+            side = jnp.where((line_row == 7 - h) & (lane // 32 == j), spread(side_slots, h * group + j, 0), side)
+    sides[y, own_at, :] = side
+    send_plane(2)
+
+    all_slots(rhs_slots, 1).wait_recv()
+    unpick = 32 * (line_row // 2) + lane % 32
+    for h in range(per_line):
         value = None
         for j in range(group):
-            slot = slots[h * group + j]
-            shift = (32 * (j - k)) % LANES
-            moved = pltpu.roll(slot, shift, 1) if shift else slot
+            both_rows = jnp.where(line_row % 2 == 0, spread(rhs_slots, h * group + j, 0), spread(rhs_slots, h * group + j, 1))
+            moved = jnp.take_along_axis(both_rows, unpick, axis=1)
             value = moved if value is None else jnp.where(lane // 32 == j, moved, value)
-        return value
-
-    own_at = pl.ds(pl.multiple_of(PAD + la * own_rows, 8), own_rows)
-    all_slots(face_slots, 0).wait_recv()
-    for h in range(per_line):
-        for k in range(3):
-            faces[k, y * per_line + h, own_at, :] = gathered(face_slots, h, k)
-    send_plane(0)
-    all_slots(rhs_slots, 1).wait_recv()
-    edge = None
-    for j in range(ring):
-        moved = pltpu.roll(rhs_slots[j], LANES // 2, 1) if 8 * j < LANES // 2 else rhs_slots[j]
-        edge = moved if edge is None else jnp.where(lane // 8 == j, moved, edge)
-    for h in range(per_line):
-        rhs[y * (per_line + 1) + h, own_at, :] = gathered(rhs_slots, h, 0)
-        north = gathered(rhs_slots, h, 1)
-        edge = jnp.where(line_row == 7 - h, pltpu.roll(north, 8 - h, 0) if h else north, edge)
-    rhs[y * (per_line + 1) + per_line, own_at, :] = edge
+        rhs[y * per_line + h, own_at, :] = value
     send_plane(1)
-    take_plane(0)
+    take_bulk(0)
+    take_bulk(2)
     take_plane(1)
 
     height = lat_count * own_rows
@@ -502,43 +618,40 @@
     west_face, diagonal = bottom.at[1], bottom.at[2]
     rest_ref, image_ref, along_ref = bottom.at[0], bottom.at[3], bottom.at[4]
     all_passed(0).wait_recv()
-    all_passed(1).wait_recv()
-
-    def rhs_tile(t):
-        return t // per_line * (per_line + 1) + t % per_line
-
-    sent(0)
+    all_passed(2).wait_recv()
+    east_face, north_face = bottom.at[5], bottom.at[6]
     lane_lat = lane_of(lat_count)
     for t in range(tiles):
-        h, edge_tile = t % per_line, t // per_line * (per_line + 1) + per_line
-        side = pl.ds(PAD + 7, lat_count, stride=8)
-        faces[1, t, side, :] = rhs[edge_tile, pl.ds(PAD + 7 - h, lat_count, stride=8), :]
-        east = rhs[edge_tile, pl.ds(PAD, lat_count, stride=8), :]
+        h, line = t % per_line, t // per_line
+        north_face[t, everything, :] = faces[1, t, everything, :]
+        north_face[t, pl.ds(PAD + 7, lat_count, stride=8), :] = sides[line, pl.ds(PAD + 7 - h, lat_count, stride=8), :]
+        east = sides[line, pl.ds(PAD, lat_count, stride=8), :]
         for row in range(own_rows):
             at = pl.ds(PAD + row, lat_count, stride=8)
             moved = jnp.take_along_axis(east, 8 * (h * group + lane_lat // 32) + row, axis=1)
-            faces[0, t, at, :] = jnp.where(lane_lat % 32 == 31, moved, faces[0, t, at, :])
+            east_face[t, at, :] = jnp.where(lane_lat % 32 == 31, moved, faces[0, t, at, :])
     for t in range(tiles):
-        east = faces[0, t, everything, :]
-        before = faces[0, (t - 1) % tiles, everything, :]
+        east = east_face[t, everything, :]
+        before = east_face[(t - 1) % tiles, everything, :]
         west = pltpu.roll(jnp.where(lane3 >= LANES - 1, before, east), 1, 1)
         west_face[t, everything, :] = west
         diagonal[t, everything, :] = (
             faces[2, t, everything, :] + east + west
-            + faces[1, t, everything, :] + faces[1, t, pl.ds(PAD - 1, height), :]
-        )
-
-    def operate(ref, place):
+            + north_face[t, everything, :] + north_face[t, pl.ds(PAD - 1, height), :]
+        )
+    all_passed(1).wait_recv()
+
+    def operate(ref):
         norm, product = None, None
         for t in range(tiles):
-            value = ref[place(t), everything, :]
-            east = pltpu.roll(jnp.where(lane3 < 1, ref[place((t + 1) % tiles), everything, :], value), LANES - 1, 1)
-            west = pltpu.roll(jnp.where(lane3 >= LANES - 1, ref[place((t - 1) % tiles), everything, :], value), 1, 1)
+            value = ref[t, everything, :]
+            east = pltpu.roll(jnp.where(lane3 < 1, ref[(t + 1) % tiles, everything, :], value), LANES - 1, 1)
+            west = pltpu.roll(jnp.where(lane3 >= LANES - 1, ref[(t - 1) % tiles, everything, :], value), 1, 1)
             image = diagonal[t, everything, :] * value - (
-                faces[0, t, everything, :] * east
+                east_face[t, everything, :] * east
                 + west_face[t, everything, :] * west
-                + faces[1, t, everything, :] * ref[place(t), pl.ds(PAD + 1, height), :]
-                + faces[1, t, pl.ds(PAD - 1, height), :] * ref[place(t), pl.ds(PAD - 1, height), :]
+                + north_face[t, everything, :] * ref[t, pl.ds(PAD + 1, height), :]
+                + north_face[t, pl.ds(PAD - 1, height), :] * ref[t, pl.ds(PAD - 1, height), :]
             )
             image_ref[t, everything, :] = image
             square, mixed = value * value, value * image
@@ -551,13 +664,13 @@
     near = pl.ds(pl.multiple_of(la * own_rows, 8), 2 * PAD + own_rows)
     solved = [None] * 3
     direction = [None] * 3
-    norm, product = operate(rhs, rhs_tile)
+    norm, product = operate(rhs)
     alpha = norm / product
     beta = None
     for iteration in range(BOTTOM_ITERS):
-        current, tile_at = (rhs, rhs_tile) if iteration == 0 else (rest_ref, lambda t: t)
+        current = rhs if iteration == 0 else rest_ref
         for k in range(3):
-            value = current[tile_at(near_tiles[k]), near, :]
+            value = current[near_tiles[k], near, :]
             direction[k] = value if iteration == 0 else value + beta * direction[k]
             solved[k] = alpha * direction[k] if iteration == 0 else solved[k] + alpha * direction[k]
         if iteration == BOTTOM_ITERS - 1:
@@ -567,8 +680,8 @@
             if iteration:
                 along = along + beta * along_ref[t, everything, :]
             along_ref[t, everything, :] = along
-            rest_ref[t, everything, :] = current[tile_at(t), everything, :] - alpha * along
-        norm_next, product = operate(rest_ref, lambda t: t)
+            rest_ref[t, everything, :] = current[t, everything, :] - alpha * along
+        norm_next, product = operate(rest_ref)
         beta = norm_next / norm
         alpha = norm_next / (product - beta * norm_next / alpha)
         norm = norm_next
@@ -603,11 +716,11 @@
             top.tmp.at[c, pl.ds(PAD + RIM, ROWS), :], residual_out.at[:, pl.ds(c * LANES, LANES)], out_sem))
         stores[-1].start()
 
-    for dy, dx in order:
-        where_inside(dy, lambda dy=dy, dx=dx: rim_copy(dy, dx).wait_send())
-    for which, slots in enumerate((face_slots, rhs_slots)):
+    for k in range(3):
+        all_rims(k, lambda copy: copy.wait_send())
+    for which, slots in enumerate((face_slots, rhs_slots, side_slots)):
         all_slots(slots, which).wait_send()
-    sent(1)
+        sent(which)
     for store in stores:
         store.wait()
 
@@ -630,39 +743,48 @@
     height = lat_count * (ROWS >> 3) + 2 * PAD
     f32 = jnp.float32
 
-    def padded(level):
-        return pltpu.VMEM((3, ((ROWS + 2 * RIM) >> level) + 2 * PAD, LANES), f32)
+    def padded(level, rim=RIM):
+        return pltpu.VMEM((3, ((ROWS + 2 * rim) >> level) + 2 * PAD, LANES), f32)
 
     rows = ROWS + 2 * RIM
     scratch = [
         pltpu.VMEM((2, 2, ROWS, LANES), f32),
         pltpu.VMEM((2, 2, ROWS, LANES), jnp.int32),
         pltpu.VMEM((3, 3, rows + 2 * PAD, LANES), f32),
-        *[padded(0)] * 7,
+        *[padded(0)] * 8,
         *[padded(1)] * 10,
         *[padded(2)] * 10,
+        pltpu.VMEM((3, 3, ROWS + 2 * NEAR + 2 * PAD, LANES), f32),
+        *[padded(0, NEAR)] * 8,
+        *[padded(1, NEAR)] * 10,
+        *[padded(2, NEAR)] * 10,
         pltpu.VMEM((ROWS, LANES), f32),
         pltpu.VMEM((ROWS, LANES), f32),
         pltpu.VMEM((rows, LANES), f32),
         pltpu.VMEM((rows, LANES), f32),
+        pltpu.VMEM((2, ROWS // 2, LANES), f32),
+        pltpu.VMEM((2, ROWS // 2, LANES), f32),
+        pltpu.VMEM((2, 2, NEAR, LANES), f32),
         pltpu.VMEM((2, rows, LANES), f32),
         pltpu.VMEM((ring, 8, LANES), f32),
-        pltpu.VMEM((ring, 8, LANES), f32),
+        pltpu.VMEM((ring, 2, LANES), f32),
+        pltpu.VMEM((ring, 2, LANES), f32),
         pltpu.VMEM((3, tiles, height, LANES), f32),
-        pltpu.VMEM((tiles + lon_count // ring, height, LANES), f32),
-        pltpu.VMEM((5, tiles, height, LANES), f32),
-        padded(0),
+        pltpu.VMEM((tiles, height, LANES), f32),
+        pltpu.VMEM((lon_count // ring, height, LANES), f32),
+        pltpu.VMEM((7, tiles, height, LANES), f32),
         pltpu.VMEM((3, 2 * PAD + (ROWS >> 3), LANES), f32),
         pltpu.SemaphoreType.DMA,
         pltpu.SemaphoreType.DMA,
-        pltpu.SemaphoreType.DMA((8,)),
-        pltpu.SemaphoreType.DMA((8,)),
+        pltpu.SemaphoreType.DMA((3,)),
+        pltpu.SemaphoreType.DMA((3,)),
+        pltpu.SemaphoreType.DMA((3,)),
+        pltpu.SemaphoreType.DMA((3,)),
+        pltpu.SemaphoreType.DMA((3,)),
         pltpu.SemaphoreType.DMA((2,)),
-        pltpu.SemaphoreType.DMA((2,)),
-        pltpu.SemaphoreType.DMA((2, planes)),
-        pltpu.SemaphoreType.DMA((2, planes)),
-        pltpu.SemaphoreType.DMA((2,)),
-        pltpu.SemaphoreType.DMA((2,)),
+        pltpu.SemaphoreType.DMA((planes - 1,)),
+        pltpu.SemaphoreType.DMA((3,)),
+        pltpu.SemaphoreType.DMA((3,)),
     ]
 
     def step(forcing, surface_term, sea_cells, levels):

time: 33.4 us -> 32.5 us (0.973)
  Pallas kernels: 32.6 us -> 31.7 us
    pallas_call x1, Pallas kernels: 31.9 us -> 31 us  [step(): pl.pallas_call(functools.partial(body, (lat_count, lon_count, ring)), out...]
where the time goes in v3:
time: 32.5 us; the launch traced here: 32.3 us
  Pallas kernels  31.7 us (98%)
  between operations  0.64 us (2%)
    pallas_call x1, Pallas kernels, step(): pl.pallas_call(functools.partial(body, (lat_count, lon_count, ring)), out...  31 us
    pallas_call x1, Pallas kernels, step(): pl.pallas_call(put_out, out_shape=(out, out), in_specs=[pl.BlockSpec(memo...  0.67 us

profile of v3, /device:TPU:1, one launch (start us, length us, event | category | flops | bytes accessed | tf_op | source)
XLA Modules:
  0.0 32.3 jit_solution(1670600653063487404)
XLA Ops:
  0.6 31.0 %shard_map.59 = (f32[64,256]{1,0:T(8,128)S(1)}, f32[64,256]{1,0:T(8,128)S(1)}) custom-call(f32[64,256]{1,0:T(8,128)} %forcing.1, f32[64,256]{1,0:T(8,128)} %surface.1, s32[64,256]{1,0:T(8,128)} %sea.1, s32[64,256]{1,0:T(8,128)} %depth_levels.1), custom_call_target="tpu_custom_call" | custom-call | tf_op jit(solution)/shard_map/pallas_call | solution.py:792
  31.7 0.7 %shard_map.60 = (f32[64,256]{1,0:T(8,128)}, f32[64,256]{1,0:T(8,128)}) custom-call(f32[64,256]{1,0:T(8,128)S(1)} %get-tuple-element.4.solution_in, f32[64,256]{1,0:T(8,128)S(1)} %get-tuple-element.5.residual_in), custom_call_target="tpu_custom_call" | custom-call | tf_op jit(solution)/shard_map/pallas_call | solution.py:802

commit v4 on v3

--- a/solution.py
+++ b/solution.py
@@ -94,14 +94,12 @@
             out.append(self.load(self.diag, c, row, count) * value[c] - around)
         return value, out
 
-    def smooth(self, source_ref, target_ref):
-        for row in self.chunks():
-            value, image = self.apply(source_ref, row, self.chunk)
+    def smooth(self, source_ref, target_ref, chunks=None):
+        for row, n in chunks or [(row, self.chunk) for row in self.chunks()]:
+            value, image = self.apply(source_ref, row, n)
             for c in range(3):
-                rest = self.load(self.rhs, c, row, self.chunk) - image[c]
-                target_ref[c, pl.ds(PAD + row, self.chunk), :] = (
-                    value[c] + self.load(self.scale, c, row, self.chunk) * rest
-                )
+                rest = self.load(self.rhs, c, row, n) - image[c]
+                target_ref[c, pl.ds(PAD + row, n), :] = value[c] + self.load(self.scale, c, row, n) * rest
 
     def finish(self):
         n = self.chunk
@@ -151,17 +149,19 @@
                 self.tmp[c, pl.ds(PAD + row, n), :] = self.load(self.rhs, c, row, n) - image[c]
 
     def rise(self, coarse, offset, masked):
-        half = self.rows // 2
-        n = min(CHUNK, half)
-        for row in range(0, half, n):
+        begin = (self.rim - 4) // 8 * 8
+        count = self.rows - 2 * begin
+        n = next(n for n in (32, 24, 16) if count % n == 0)
+        for row in range(begin // 2, (begin + count) // 2, n // 2):
             for c in range(3):
-                added = coarse[c, pl.ds(offset + row, n), :]
+                added = coarse[c, pl.ds(offset + row, n // 2), :]
                 for odd in range(2):
-                    at = pl.ds(PAD + 2 * row + odd, n, stride=2)
+                    at = pl.ds(PAD + 2 * row + odd, n // 2, stride=2)
                     own = jnp.where(self.source[c, at, :] > 0.0, added, 0.0) if masked else added
                     self.va[c, at, :] = self.va[c, at, :] + own
-        self.smooth(self.va, self.vb)
-        self.smooth(self.vb, self.va)
+        chunks = [(row, n) for row in range(begin, begin + count, n)]
+        self.smooth(self.va, self.vb, chunks)
+        self.smooth(self.vb, self.va, chunks)
 
 
 def body(
@@ -175,7 +175,7 @@
         west_pack, east_pack, east_rim, west_rim, near_packs, near_rims, near_corners, metric,
         face_slots, rhs_slots, side_slots, faces, rhs, sides, bottom, piece,
         in_sem, out_sem, rim_send, rim_recv, slot_send, slot_recv,
-        plane_send, bulk_recv, plane_recv, pass_send, pass_recv,
+        plane_send, plane_recv, pass_send, pass_recv,
     ) = rest[57:]
     planes_y = lon_count // ring
     planes_x = lat_count // CORES
@@ -225,8 +225,8 @@
     def ring_peer(step):
         return la, y * ring + lax.rem(z + step, ring)
 
-    def plane_peer(dx, dy):
-        return lax.rem(x + dx, planes_x) * CORES + core, lax.rem(y + dy, planes_y) * ring + z
+    def plane_peer(dx, dy, other=0):
+        return lax.rem(x + dx, planes_x) * CORES + (1 - core if other else core), lax.rem(y + dy, planes_y) * ring + z
 
     partner = (x * CORES + (1 - core), lo)
     inside = {-1: la > 0, 0: None, 1: la < lat_count - 1}
@@ -242,7 +242,8 @@
     for step in ring_steps:
         greet(*ring_peer(step))
     for dx, dy in hops:
-        greet(*plane_peer(dx, dy))
+        for other in range(CORES):
+            greet(*plane_peer(dx, dy, other))
     greet(*partner)
 
     def clear(ref, col, row, count):
@@ -278,6 +279,7 @@
     for row in range(0, ROWS + 2 * RIM, CHUNK):
         number = (first + row + lax.broadcasted_iota(jnp.int32, (CHUNK, LANES), 0)).astype(jnp.float32)
         metric[0, pl.ds(row, CHUNK), :] = cosines(number + 0.5)
+        metric[2, pl.ds(row, CHUNK), :] = 1.0 / metric[0, pl.ds(row, CHUNK), :]
         metric[1, pl.ds(row, CHUNK), :] = cosines(number + 1.0)
 
     for load in loads:
@@ -339,7 +341,7 @@
     for row in range(8):
         deep = [every8(0, c, row) for c in range(2)]
         east = east_of(deep, 1, lane)
-        inverse = 1.0 / metric[0, pl.ds(RIM + row, own_rows, stride=8), :]
+        inverse = metric[2, pl.ds(RIM + row, own_rows, stride=8), :]
         for c in range(2):
             face, term = jnp.minimum(deep[c], east[c]) * inverse, every8(2, c, row)
             sums[0][c] = face if row == 0 else sums[0][c] + face
@@ -352,7 +354,7 @@
     parts = [dense(*sums[0], last=7), dense(*sums[1]), dense(*sums[2])]
     face_slots[z] = jnp.where(lane < 32, parts[0], jnp.where(lane < 64, parts[1], parts[2]))
 
-    greeted = 2 + (ring - 1) + len(hops) + 1
+    greeted = 2 + (ring - 1) + CORES * len(hops) + 1
     both = inside[-1].astype(jnp.int32) + inside[1].astype(jnp.int32)
     pl.semaphore_wait(barrier, greeted + 3 * both)
 
@@ -424,20 +426,20 @@
             return rhs.at[pl.ds(line * per_line, per_line), rows, :]
         return sides.at[line, rows, :]
 
-    def plane_copy(which, k, dx, dy):
+    def plane_copy(which, dx, dy, other):
         block = plane_block(which, la, y)
         return pltpu.make_async_remote_copy(
-            block, block, plane_send.at[which], plane_recv.at[k] if which == 1 else bulk_recv.at[which // 2],
-            device_id=device(*plane_peer(dx, dy)), device_id_type=MESH,
+            block, block, plane_send.at[which], plane_recv.at[which],
+            device_id=device(*plane_peer(dx, dy, other)), device_id_type=MESH,
         )
 
     def all_planes(which):
-        count = len(hops)
+        count = len(hops) * (CORES if which == 1 else 1)
         lines, rows = (3, count // 3 * 8) if count % 3 == 0 else (1, count * 8)
         rows, of_tiles = pl.ds(0, rows), pl.ds(0, lines * per_line)
         block = (faces.at[:, of_tiles, rows, :], rhs.at[of_tiles, rows, :], sides.at[pl.ds(0, lines), rows, :])[which]
         return pltpu.make_async_remote_copy(
-            block, block, plane_send.at[which], bulk_recv.at[which // 2],
+            block, block, plane_send.at[which], plane_recv.at[which],
             device_id=device(*partner), device_id_type=MESH,
         )
 
@@ -457,14 +459,18 @@
         )
 
     def send_plane(which):
-        for k, (dx, dy) in enumerate(hops):
-            plane_copy(which, k, dx, dy).start()
+        for dx, dy in hops:
+            for other in range(CORES if which == 1 else 1):
+                plane_copy(which, dx, dy, other).start()
         if which == 1:
             pass_copy(which, la, y).start()
 
     def sent(which):
         all_planes(which).wait_send()
-        all_passed(which).wait_send()
+        if which == 1:
+            pass_copy(1, la, y).wait_send()
+        else:
+            all_passed(which).wait_send()
 
     def take_bulk(which):
         all_planes(which).wait_recv()
@@ -476,11 +482,6 @@
                 device_id=device(*partner), device_id_type=MESH,
             ).start()
 
-    def take_plane(which):
-        for k, (dx, dy) in reversed([*enumerate(hops)]):
-            plane_copy(which, k, dx, dy).wait_recv()
-            pass_copy(which, *(lax.rem(x - dx + planes_x, planes_x) * CORES + core, lax.rem(y - dy + planes_y, planes_y))).start()
-
     order = sorted(rims, key=lambda d: (d[1] == 0, d[0] == 0))
     for dy, dx in order:
         where_inside(dy, lambda dy=dy, dx=dx: near_copy(dy, dx).start())
@@ -495,7 +496,7 @@
         for row in first.chunks():
             deep = [first.load(base.at[0], c, row, n) for c in range(3)]
             east = east_of(deep, 1, lane_of(n))
-            inverse = 1.0 / metric[0, pl.ds(RIM - first.rim + row, n), :]
+            inverse = metric[2, pl.ds(RIM - first.rim + row, n), :]
             northern = metric[1, pl.ds(RIM - first.rim + row, n), :]
             for c in range(3):
                 at = pl.ds(PAD + row, n)
@@ -610,7 +611,6 @@
     send_plane(1)
     take_bulk(0)
     take_bulk(2)
-    take_plane(1)
 
     height = lat_count * own_rows
     everything = pl.ds(PAD, height)
@@ -639,7 +639,8 @@
             faces[2, t, everything, :] + east + west
             + north_face[t, everything, :] + north_face[t, pl.ds(PAD - 1, height), :]
         )
-    all_passed(1).wait_recv()
+    all_planes(1).wait_recv()
+    pass_copy(1, la, y).wait_recv()
 
     def operate(ref):
         norm, product = None, None
@@ -738,7 +739,6 @@
 
 def solution(mesh, ring=RING):
     lat_count, lon_count = mesh.shape["lat"], mesh.shape["lon"]
-    planes = (lat_count // CORES) * (lon_count // ring)
     tiles = lon_count * (COLS >> 3) // LANES
     height = lat_count * (ROWS >> 3) + 2 * PAD
     f32 = jnp.float32
@@ -765,7 +765,7 @@
         pltpu.VMEM((2, ROWS // 2, LANES), f32),
         pltpu.VMEM((2, ROWS // 2, LANES), f32),
         pltpu.VMEM((2, 2, NEAR, LANES), f32),
-        pltpu.VMEM((2, rows, LANES), f32),
+        pltpu.VMEM((3, rows, LANES), f32),
         pltpu.VMEM((ring, 8, LANES), f32),
         pltpu.VMEM((ring, 2, LANES), f32),
         pltpu.VMEM((ring, 2, LANES), f32),
@@ -781,8 +781,7 @@
         pltpu.SemaphoreType.DMA((3,)),
         pltpu.SemaphoreType.DMA((3,)),
         pltpu.SemaphoreType.DMA((3,)),
-        pltpu.SemaphoreType.DMA((2,)),
-        pltpu.SemaphoreType.DMA((planes - 1,)),
+        pltpu.SemaphoreType.DMA((3,)),
         pltpu.SemaphoreType.DMA((3,)),
         pltpu.SemaphoreType.DMA((3,)),
     ]

time: 32.5 us -> 32.2 us (level)
  no operation moved by 1% of the time
where the time goes in v4:
time: 32.2 us; the launch traced here: 32 us
  Pallas kernels  31.4 us (98%)
  between operations  0.64 us (2%)
    pallas_call x1, Pallas kernels, step(): pl.pallas_call(functools.partial(body, (lat_count, lon_count, ring)), out...  30.7 us
    pallas_call x1, Pallas kernels, step(): pl.pallas_call(put_out, out_shape=(out, out), in_specs=[pl.BlockSpec(memo...  0.67 us

profile of v4, /device:TPU:1, one launch (start us, length us, event | category | flops | bytes accessed | tf_op | source)
XLA Modules:
  0.0 32.0 jit_solution(3680167168739692576)
XLA Ops:
  0.6 30.7 %shard_map.59 = (f32[64,256]{1,0:T(8,128)S(1)}, f32[64,256]{1,0:T(8,128)S(1)}) custom-call(f32[64,256]{1,0:T(8,128)} %forcing.1, f32[64,256]{1,0:T(8,128)} %surface.1, s32[64,256]{1,0:T(8,128)} %sea.1, s32[64,256]{1,0:T(8,128)} %depth_levels.1), custom_call_target="tpu_custom_call" | custom-call | tf_op jit(solution)/shard_map/pallas_call | solution.py:791
  31.4 0.7 %shard_map.60 = (f32[64,256]{1,0:T(8,128)}, f32[64,256]{1,0:T(8,128)}) custom-call(f32[64,256]{1,0:T(8,128)S(1)} %get-tuple-element.4.solution_in, f32[64,256]{1,0:T(8,128)S(1)} %get-tuple-element.5.residual_in), custom_call_target="tpu_custom_call" | custom-call | tf_op jit(solution)/shard_map/pallas_call | solution.py:801

commit v5 on v4

--- a/solution.py
+++ b/solution.py
@@ -70,7 +70,7 @@
         self.rows = (ROWS + 2 * rim) >> index
         self.rim = rim >> index
         self.east, self.west, self.north, self.source, self.diag, self.scale, self.rhs, self.va, self.vb, self.tmp = refs
-        self.chunk = next(n for n in (32, 24, 16, 8) if self.rows % n == 0)
+        self.chunk = next(n for n in (16, 8) if self.rows % n == 0)
 
     def chunks(self):
         return range(0, self.rows, self.chunk)
@@ -151,7 +151,7 @@
     def rise(self, coarse, offset, masked):
         begin = (self.rim - 4) // 8 * 8
         count = self.rows - 2 * begin
-        n = next(n for n in (32, 24, 16) if count % n == 0)
+        n = 16
         for row in range(begin // 2, (begin + count) // 2, n // 2):
             for c in range(3):
                 added = coarse[c, pl.ds(offset + row, n // 2), :]
@@ -205,9 +205,6 @@
     for k, ref in enumerate((sea, depth_levels)):
         for c in range(2):
             loads.append(pltpu.make_async_copy(ref.at[:, pl.ds(c * LANES, LANES)], in_i.at[k, c], in_sem))
-    for load in loads:
-        load.start()
-
     rims = [(dy, dx) for dy in (-1, 0, 1) for dx in (-1, 0, 1) if (dy, dx) != (0, 0)]
     hops = sorted(
         ((dx, dy) for dx in range(planes_x) for dy in range(planes_y) if (dx, dy) != (0, 0)),
@@ -237,14 +234,15 @@
         else:
             pl.when(inside[dy])(act)
 
-    for dy, dx in rims:
-        where_inside(dy, lambda dy=dy, dx=dx: greet(*beside(dy, dx)))
-    for step in ring_steps:
-        greet(*ring_peer(step))
     for dx, dy in hops:
         for other in range(CORES):
             greet(*plane_peer(dx, dy, other))
-    greet(*partner)
+    for step in ring_steps:
+        greet(*ring_peer(step))
+    for dy, dx in sorted(rims, key=lambda d: (d[1] == 0, d[0] == 0)):
+        where_inside(dy, lambda dy=dy, dx=dx: greet(*beside(dy, dx)))
+    for load in loads:
+        load.start()
 
     def clear(ref, col, row, count):
         ref[col, pl.ds(row, count), :] = jnp.zeros((count, LANES), ref.dtype)
@@ -258,7 +256,7 @@
                 for ref in (level.north, level.va, level.vb):
                     clear(ref, c, 0, PAD)
                     clear(ref, c, PAD + level.rows, PAD)
-    for ref in (faces.at[1], rhs, bottom.at[0], bottom.at[6]):
+    for ref in (faces.at[1], rhs, bottom.at[0], bottom.at[3], bottom.at[6]):
         for t in range(tiles):
             clear(ref, t, 0, PAD)
             clear(ref, t, PAD + lat_count * own_rows, PAD)
@@ -354,7 +352,7 @@
     parts = [dense(*sums[0], last=7), dense(*sums[1]), dense(*sums[2])]
     face_slots[z] = jnp.where(lane < 32, parts[0], jnp.where(lane < 64, parts[1], parts[2]))
 
-    greeted = 2 + (ring - 1) + CORES * len(hops) + 1
+    greeted = 2 + (ring - 1) + CORES * len(hops)
     both = inside[-1].astype(jnp.int32) + inside[1].astype(jnp.int32)
     pl.semaphore_wait(barrier, greeted + 3 * both)
 
@@ -617,6 +615,7 @@
     lane3 = lane_of(height)
     west_face, diagonal = bottom.at[1], bottom.at[2]
     rest_ref, image_ref, along_ref = bottom.at[0], bottom.at[3], bottom.at[4]
+    image_image, far_ref = bottom.at[7], bottom.at[8]
     all_passed(0).wait_recv()
     all_passed(2).wait_recv()
     east_face, north_face = bottom.at[5], bottom.at[6]
@@ -642,50 +641,73 @@
     all_planes(1).wait_recv()
     pass_copy(1, la, y).wait_recv()
 
-    def operate(ref):
+    part = 16
+    lane3 = lane_of(part)
+    pieces = [(t, row) for t in range(tiles) for row in range(PAD, PAD + height, part)]
+
+    def add(total, value):
+        return value if total is None else total + value
+
+    def operate(ref, target, sums):
         norm, product = None, None
-        for t in range(tiles):
-            value = ref[t, everything, :]
-            east = pltpu.roll(jnp.where(lane3 < 1, ref[(t + 1) % tiles, everything, :], value), LANES - 1, 1)
-            west = pltpu.roll(jnp.where(lane3 >= LANES - 1, ref[(t - 1) % tiles, everything, :], value), 1, 1)
-            image = diagonal[t, everything, :] * value - (
-                east_face[t, everything, :] * east
-                + west_face[t, everything, :] * west
-                + north_face[t, everything, :] * ref[t, pl.ds(PAD + 1, height), :]
-                + north_face[t, pl.ds(PAD - 1, height), :] * ref[t, pl.ds(PAD - 1, height), :]
+        for t, row in pieces:
+            at = pl.ds(row, part)
+            value = ref[t, at, :]
+            east = pltpu.roll(jnp.where(lane3 < 1, ref[(t + 1) % tiles, at, :], value), LANES - 1, 1)
+            west = pltpu.roll(jnp.where(lane3 >= LANES - 1, ref[(t - 1) % tiles, at, :], value), 1, 1)
+            image = diagonal[t, at, :] * value - (
+                east_face[t, at, :] * east
+                + west_face[t, at, :] * west
+                + north_face[t, at, :] * ref[t, pl.ds(row + 1, part), :]
+                + north_face[t, pl.ds(row - 1, part), :] * ref[t, pl.ds(row - 1, part), :]
             )
-            image_ref[t, everything, :] = image
-            square, mixed = value * value, value * image
-            norm = square if norm is None else norm + square
-            product = mixed if product is None else product + mixed
-        return jnp.sum(norm, keepdims=True), jnp.sum(product, keepdims=True)
+            target[t, at, :] = image
+            if sums:
+                norm, product = add(norm, value * value), add(product, value * image)
+        if sums:
+            return jnp.sum(norm, keepdims=True), jnp.sum(product, keepdims=True)
 
     own_tile = lo // group
     near_tiles = (lax.rem(own_tile - 1 + tiles, tiles), own_tile, lax.rem(own_tile + 1, tiles))
     near = pl.ds(pl.multiple_of(la * own_rows, 8), 2 * PAD + own_rows)
     solved = [None] * 3
     direction = [None] * 3
-    norm, product = operate(rhs)
-    alpha = norm / product
+    norm, product = operate(rhs, image_ref, True)
     beta = None
     for iteration in range(BOTTOM_ITERS):
+        final = iteration == BOTTOM_ITERS - 1
         current = rhs if iteration == 0 else rest_ref
+        if not final:
+            operate(image_ref, image_image, False)
+        if iteration:
+            beta = norm * inverse_norm
+            product = product - beta * norm * inverse_alpha
+        alpha = norm / product
+        inverse_norm = 1.0 / norm
+        inverse_alpha = product * inverse_norm
         for k in range(3):
             value = current[near_tiles[k], near, :]
             direction[k] = value if iteration == 0 else value + beta * direction[k]
             solved[k] = alpha * direction[k] if iteration == 0 else solved[k] + alpha * direction[k]
-        if iteration == BOTTOM_ITERS - 1:
+        if final:
             break
-        for t in range(tiles):
-            along = image_ref[t, everything, :]
+        norm, product = None, None
+        for t, row in pieces:
+            at = pl.ds(row, part)
+            image = image_ref[t, at, :]
+            along, far = image, image_image[t, at, :]
             if iteration:
-                along = along + beta * along_ref[t, everything, :]
-            along_ref[t, everything, :] = along
-            rest_ref[t, everything, :] = current[t, everything, :] - alpha * along
-        norm_next, product = operate(rest_ref)
-        beta = norm_next / norm
-        alpha = norm_next / (product - beta * norm_next / alpha)
-        norm = norm_next
+                along = along + beta * along_ref[t, at, :]
+                far = far + beta * far_ref[t, at, :]
+            rest = current[t, at, :] - alpha * along
+            image = image - alpha * far
+            rest_ref[t, at, :] = rest
+            if iteration < BOTTOM_ITERS - 2:
+                along_ref[t, at, :] = along
+                far_ref[t, at, :] = far
+                image_ref[t, at, :] = image
+            norm, product = add(norm, rest * rest), add(product, rest * image)
+        norm, product = jnp.sum(norm, keepdims=True), jnp.sum(product, keepdims=True)
 
     quarter = (lo % group) * 32
     lane = lane_of(8)
@@ -772,7 +794,7 @@
         pltpu.VMEM((3, tiles, height, LANES), f32),
         pltpu.VMEM((tiles, height, LANES), f32),
         pltpu.VMEM((lon_count // ring, height, LANES), f32),
-        pltpu.VMEM((7, tiles, height, LANES), f32),
+        pltpu.VMEM((9, tiles, height, LANES), f32),
         pltpu.VMEM((3, 2 * PAD + (ROWS >> 3), LANES), f32),
         pltpu.SemaphoreType.DMA,
         pltpu.SemaphoreType.DMA,

time: 32.2 us -> 31.9 us (level)
    pallas_call x1, Pallas kernels: 30.7 us -> 30.4 us  [step(): pl.pallas_call(functools.partial(body, (lat_count, lon_count, ring)), out...]
where the time goes in v5:
time: 31.9 us; the launch traced here: 31.7 us
  Pallas kernels  31.1 us (97%)
  between operations  0.64 us (2%)
    pallas_call x1, Pallas kernels, step(): pl.pallas_call(functools.partial(body, (lat_count, lon_count, ring)), out...  30.4 us
    pallas_call x1, Pallas kernels, step(): pl.pallas_call(put_out, out_shape=(out, out), in_specs=[pl.BlockSpec(memo...  0.67 us

profile of v5, /device:TPU:1, one launch (start us, length us, event | category | flops | bytes accessed | tf_op | source)
XLA Modules:
  0.0 31.7 jit_solution(17628630482951644363)
XLA Ops:
  0.6 30.4 %shard_map.59 = (f32[64,256]{1,0:T(8,128)S(1)}, f32[64,256]{1,0:T(8,128)S(1)}) custom-call(f32[64,256]{1,0:T(8,128)} %forcing.1, f32[64,256]{1,0:T(8,128)} %surface.1, s32[64,256]{1,0:T(8,128)} %sea.1, s32[64,256]{1,0:T(8,128)} %depth_levels.1), custom_call_target="tpu_custom_call" | custom-call | tf_op jit(solution)/shard_map/pallas_call | solution.py:813
  31.0 0.7 %shard_map.60 = (f32[64,256]{1,0:T(8,128)}, f32[64,256]{1,0:T(8,128)}) custom-call(f32[64,256]{1,0:T(8,128)S(1)} %get-tuple-element.4.solution_in, f32[64,256]{1,0:T(8,128)S(1)} %get-tuple-element.5.residual_in), custom_call_target="tpu_custom_call" | custom-call | tf_op jit(solution)/shard_map/pallas_call | solution.py:823

commit v6 on v5

--- a/solution.py
+++ b/solution.py
@@ -235,8 +235,7 @@
             pl.when(inside[dy])(act)
 
     for dx, dy in hops:
-        for other in range(CORES):
-            greet(*plane_peer(dx, dy, other))
+        greet(*plane_peer(dx, dy))
     for step in ring_steps:
         greet(*ring_peer(step))
     for dy, dx in sorted(rims, key=lambda d: (d[1] == 0, d[0] == 0)):
@@ -352,7 +351,7 @@
     parts = [dense(*sums[0], last=7), dense(*sums[1]), dense(*sums[2])]
     face_slots[z] = jnp.where(lane < 32, parts[0], jnp.where(lane < 64, parts[1], parts[2]))
 
-    greeted = 2 + (ring - 1) + CORES * len(hops)
+    greeted = 2 + (ring - 1) + len(hops)
     both = inside[-1].astype(jnp.int32) + inside[1].astype(jnp.int32)
     pl.semaphore_wait(barrier, greeted + 3 * both)
 
@@ -424,20 +423,23 @@
             return rhs.at[pl.ds(line * per_line, per_line), rows, :]
         return sides.at[line, rows, :]
 
-    def plane_copy(which, dx, dy, other):
+    groups = [hops[0:5], hops[5:11], hops[11:]] if len(hops) == 15 else [hops]
+
+    def plane_copy(which, dx, dy):
         block = plane_block(which, la, y)
+        group_at = [g for g, group_hops in enumerate(groups) if (dx, dy) in group_hops][0]
         return pltpu.make_async_remote_copy(
-            block, block, plane_send.at[which], plane_recv.at[which],
-            device_id=device(*plane_peer(dx, dy, other)), device_id_type=MESH,
+            block, block, plane_send.at[which], plane_recv.at[which, group_at],
+            device_id=device(*plane_peer(dx, dy)), device_id_type=MESH,
         )
 
     def all_planes(which):
-        count = len(hops) * (CORES if which == 1 else 1)
+        count = len(hops)
         lines, rows = (3, count // 3 * 8) if count % 3 == 0 else (1, count * 8)
         rows, of_tiles = pl.ds(0, rows), pl.ds(0, lines * per_line)
         block = (faces.at[:, of_tiles, rows, :], rhs.at[of_tiles, rows, :], sides.at[pl.ds(0, lines), rows, :])[which]
         return pltpu.make_async_remote_copy(
-            block, block, plane_send.at[which], plane_recv.at[which],
+            block, block, plane_send.at[which], plane_recv.at[which, 0],
             device_id=device(*partner), device_id_type=MESH,
         )
 
@@ -458,27 +460,26 @@
 
     def send_plane(which):
         for dx, dy in hops:
-            for other in range(CORES if which == 1 else 1):
-                plane_copy(which, dx, dy, other).start()
-        if which == 1:
-            pass_copy(which, la, y).start()
+            plane_copy(which, dx, dy).start()
+        pass_copy(which, la, y).start()
 
     def sent(which):
         all_planes(which).wait_send()
-        if which == 1:
-            pass_copy(1, la, y).wait_send()
-        else:
-            all_passed(which).wait_send()
-
-    def take_bulk(which):
-        all_planes(which).wait_recv()
-        for line in range(planes_x):
-            rows = pl.ds(pl.multiple_of(PAD + (line * CORES + core) * own_rows, 8), own_rows)
-            block = faces.at[:, :, rows, :] if which == 0 else sides.at[:, rows, :]
+        all_passed(which).wait_send()
+
+    def take(which):
+        for g, group_hops in enumerate(groups):
+            rows = pl.ds(0, len(group_hops) * own_rows)
+            line = pl.ds(0, per_line)
+            block = (faces.at[:, line, rows, :], rhs.at[line, rows, :], sides.at[0, rows, :])[which]
             pltpu.make_async_remote_copy(
-                block, block, pass_send.at[which], pass_recv.at[which],
+                block, block, plane_send.at[which], plane_recv.at[which, g],
                 device_id=device(*partner), device_id_type=MESH,
-            ).start()
+            ).wait_recv()
+            for dx, dy in group_hops:
+                pass_copy(
+                    which, lax.rem(x - dx + planes_x, planes_x) * CORES + core, lax.rem(y - dy + planes_y, planes_y)
+                ).start()
 
     order = sorted(rims, key=lambda d: (d[1] == 0, d[0] == 0))
     for dy, dx in order:
@@ -607,8 +608,9 @@
             value = moved if value is None else jnp.where(lane // 32 == j, moved, value)
         rhs[y * per_line + h, own_at, :] = value
     send_plane(1)
-    take_bulk(0)
-    take_bulk(2)
+    take(0)
+    take(2)
+    take(1)
 
     height = lat_count * own_rows
     everything = pl.ds(PAD, height)
@@ -638,8 +640,7 @@
             faces[2, t, everything, :] + east + west
             + north_face[t, everything, :] + north_face[t, pl.ds(PAD - 1, height), :]
         )
-    all_planes(1).wait_recv()
-    pass_copy(1, la, y).wait_recv()
+    all_passed(1).wait_recv()
 
     part = 16
     lane3 = lane_of(part)
@@ -798,14 +799,9 @@
         pltpu.VMEM((3, 2 * PAD + (ROWS >> 3), LANES), f32),
         pltpu.SemaphoreType.DMA,
         pltpu.SemaphoreType.DMA,
-        pltpu.SemaphoreType.DMA((3,)),
-        pltpu.SemaphoreType.DMA((3,)),
-        pltpu.SemaphoreType.DMA((3,)),
-        pltpu.SemaphoreType.DMA((3,)),
-        pltpu.SemaphoreType.DMA((3,)),
-        pltpu.SemaphoreType.DMA((3,)),
-        pltpu.SemaphoreType.DMA((3,)),
-        pltpu.SemaphoreType.DMA((3,)),
+        *[pltpu.SemaphoreType.DMA((3,))] * 5,
+        pltpu.SemaphoreType.DMA((3, 3)),
+        *[pltpu.SemaphoreType.DMA((3,))] * 2,
     ]
 
     def step(forcing, surface_term, sea_cells, levels):

time: 31.9 us -> 32 us (level)
  no operation moved by 1% of the time
where the time goes in v6:
time: 32 us; the launch traced here: 31.9 us
  Pallas kernels  31.2 us (98%)
  between operations  0.64 us (2%)
    pallas_call x1, Pallas kernels, step(): pl.pallas_call(functools.partial(body, (lat_count, lon_count, ring)), out...  30.6 us
    pallas_call x1, Pallas kernels, step(): pl.pallas_call(put_out, out_shape=(out, out), in_specs=[pl.BlockSpec(memo...  0.67 us

profile of v6, /device:TPU:1, one launch (start us, length us, event | category | flops | bytes accessed | tf_op | source)
XLA Modules:
  0.0 31.9 jit_solution(3058359186185873017)
XLA Ops:
  0.6 30.6 %shard_map.59 = (f32[64,256]{1,0:T(8,128)S(1)}, f32[64,256]{1,0:T(8,128)S(1)}) custom-call(f32[64,256]{1,0:T(8,128)} %forcing.1, f32[64,256]{1,0:T(8,128)} %surface.1, s32[64,256]{1,0:T(8,128)} %sea.1, s32[64,256]{1,0:T(8,128)} %depth_levels.1), custom_call_target="tpu_custom_call" | custom-call | tf_op jit(solution)/shard_map/pallas_call | solution.py:809
  31.2 0.7 %shard_map.60 = (f32[64,256]{1,0:T(8,128)}, f32[64,256]{1,0:T(8,128)}) custom-call(f32[64,256]{1,0:T(8,128)S(1)} %get-tuple-element.4.solution_in, f32[64,256]{1,0:T(8,128)S(1)} %get-tuple-element.5.residual_in), custom_call_target="tpu_custom_call" | custom-call | tf_op jit(solution)/shard_map/pallas_call | solution.py:819
